TPU v7x, 32 devices: a whole 2x2x4 slice. The times are simulated.
32 devices in a mesh: dp: 16 (over z, y, core), fsdp: 2 (over x).
Axes of the slice: x: 2, y: 2, z: 4, core: 2. Of those that a mesh axis runs over, the one named last changes fastest.
Arguments:
- frames: bfloat16 [2, 16384, 512], P(None, ('dp', 'fsdp')), may hold values from -6 to 6
- item_lengths: int32 [2, 32, 8], P(None, ('dp', 'fsdp')), may hold values from 1 to 384, 512 in all within a row
- frame_mask: int32 [2, 16384], P(None, ('dp', 'fsdp')), may hold values 0 or 1
- first_norm: bfloat16 [512], P('fsdp'), may hold values from 0.5 to 1.5
- first_up: bfloat16 [512, 2048], P('fsdp'), may hold values from -0.25 to 0.25
- first_down: bfloat16 [2048, 512], P('fsdp'), may hold values from -0.125 to 0.125
- attend_norm: bfloat16 [512], P('fsdp'), may hold values from 0.5 to 1.5
- attend_joint: bfloat16 [512, 1536], P('fsdp'), may hold values from -0.25 to 0.25
- attend_out: bfloat16 [512, 512], P('fsdp'), may hold values from -1 to 1
- conv_norm: bfloat16 [512], P('fsdp'), may hold values from 0.5 to 1.5
- conv_in: bfloat16 [512, 1024], P('fsdp'), may hold values from -0.25 to 0.25
- conv_kernel: bfloat16 [32, 512], P('fsdp'), may hold values from -1 to 1
- batch_gain: bfloat16 [512], P('fsdp'), may hold values from 0.5 to 1.5
- batch_bias: bfloat16 [512], P('fsdp'), may hold values from -3 to 3
- conv_out: bfloat16 [512, 512], P('fsdp'), may hold values from -0.25 to 0.25
- second_norm: bfloat16 [512], P('fsdp'), may hold values from 0.5 to 1.5
- second_up: bfloat16 [512, 2048], P('fsdp'), may hold values from -0.25 to 0.25
- second_down: bfloat16 [2048, 512], P('fsdp'), may hold values from -0.125 to 0.125
- final_norm: bfloat16 [512], P('fsdp'), may hold values from 0.5 to 1.5
- output_grad: bfloat16 [2, 16384, 512], P(None, ('dp', 'fsdp')), may hold values from -6 to 6
Outputs:
- encoded: bfloat16 [2, 16384, 512], P(None, ('dp', 'fsdp'))
- frames_grad: bfloat16 [2, 16384, 512], P(None, ('dp', 'fsdp'))
- first_norm_grad: float32 [512], P('fsdp')
- first_up_grad: float32 [512, 2048], P('fsdp')
- first_down_grad: float32 [2048, 512], P('fsdp')
- attend_norm_grad: float32 [512], P('fsdp')
- attend_joint_grad: float32 [512, 1536], P('fsdp')
- attend_out_grad: float32 [512, 512], P('fsdp')
- conv_norm_grad: float32 [512], P('fsdp')
- conv_in_grad: float32 [512, 1024], P('fsdp')
- conv_kernel_grad: float32 [32, 512], P('fsdp')
- batch_gain_grad: float32 [512], P('fsdp')
- batch_bias_grad: float32 [512], P('fsdp')
- conv_out_grad: float32 [512, 512], P('fsdp')
- second_norm_grad: float32 [512], P('fsdp')
- second_up_grad: float32 [512, 2048], P('fsdp')
- second_down_grad: float32 [2048, 512], P('fsdp')
- final_norm_grad: float32 [512], P('fsdp')
Inputs may be any that keep to these rules, and one draw needn't show every extreme that they name: `item_lengths`: each row of 8 lengths sums to 512; its largest is exactly 384.
All inputs are finite; a program needn't handle non-finite values. No bound on the sum of `frame_mask` on one device may be relied on, other than what follows from the above.
Results may differ from a plain program's by a relative error of at most 0.019.
Values may be sent and summed in bfloat16 or wider, within the bound.
No kernel may reach another device: no remote copies, remote signals or barrier semaphores. Data moves between devices by JAX's collectives and lax.ppermute only.
A program may use at most 192 MiB of HBM per device.

v0:
```python
import math

import jax
import jax.numpy as jnp
from jax import lax
from jax.sharding import PartitionSpec as P

HEADS = 8
KER = 32
HDIM = 64
MB = 2


EPS = 1e-05


def product(left, right):
    return jnp.dot(left, right, preferred_element_type=jnp.float32)


def product_tn(left, right):
    return lax.dot_general(
        left, right, (((0,), (0,)), ((), ())), preferred_element_type=jnp.float32
    )


def product_nt(left, right):
    return lax.dot_general(
        left, right, (((1,), (1,)), ((), ())), preferred_element_type=jnp.float32
    )


def normalize(values, gain):
    centered = values - jnp.mean(values, axis=-1, keepdims=True)
    inverse_deviation = lax.rsqrt(jnp.mean(centered * centered, axis=-1, keepdims=True) + EPS)
    normal_rows = centered * inverse_deviation
    return (normal_rows * gain, normal_rows, inverse_deviation)


def normalize_back(grad_out, normal_rows, inverse_deviation, gain):
    scaled = grad_out * gain
    grad_in = inverse_deviation * (
        scaled
        - jnp.mean(scaled, axis=-1, keepdims=True)
        - normal_rows * jnp.mean(scaled * normal_rows, axis=-1, keepdims=True)
    )
    return (grad_in, jnp.sum(grad_out * normal_rows, axis=0))


def swish_grad(values):
    gate_sigmoid = jax.nn.sigmoid(values)
    return gate_sigmoid * (1.0 + values * (1.0 - gate_sigmoid))


def frame_layout(lengths, slots):
    ends = jnp.cumsum(lengths)
    starts = ends - lengths
    slot_ids = jnp.arange(slots, dtype=jnp.int32)
    segment = jnp.sum((slot_ids[:, None] >= ends[None, :]).astype(jnp.int32), axis=1)
    member = segment[:, None] == jnp.arange(lengths.shape[0], dtype=jnp.int32)[None, :]
    begin = jnp.sum(jnp.where(member, starts[None, :], 0), axis=1)
    return (segment, slot_ids - begin)


def rotate(values, position, sign):
    half = HDIM // 2
    freq = jnp.exp(jnp.arange(half, dtype=jnp.float32) * (-2.0 * math.log(10000.0) / HDIM))
    angle = position.astype(jnp.float32)[:, None] * freq[None, :]
    cosine = jnp.cos(angle)[:, None, :]
    sine = sign * jnp.sin(angle)[:, None, :]
    first = values[..., :half]
    second = values[..., half:]
    return jnp.concatenate(
        [first * cosine - second * sine, first * sine + second * cosine], axis=-1
    )


def shifted(array, shift_by, fill):
    length = array.shape[0]
    pad_width = ((KER, KER),) + ((0, 0),) * (array.ndim - 1)
    padded = jnp.pad(array, pad_width, constant_values=fill)
    return lax.slice_in_dim(padded, KER + shift_by, KER + shift_by + length, axis=0)


def feed_forward(values, gain, w_up, w_down):
    normed, normal_rows, inverse_deviation = normalize(values, gain)
    entry_value = normed.astype(jnp.bfloat16)
    inner = product(entry_value, w_up)
    hidden = (inner * jax.nn.sigmoid(inner)).astype(jnp.bfloat16)
    return (product(hidden, w_down), (entry_value, normal_rows, inverse_deviation, inner, hidden))


def feed_back(grad_state, gain, w_up, w_down, saved_tensors):
    entry_value, normal_rows, inverse_deviation, inner, hidden = saved_tensors
    grad_branch = (0.5 * grad_state).astype(jnp.bfloat16)
    grad_down = product_tn(hidden, grad_branch)
    grad_hidden = product_nt(grad_branch, w_down)
    grad_inner = (grad_hidden * swish_grad(inner)).astype(jnp.bfloat16)
    grad_up = product_tn(entry_value, grad_inner)
    grad_entry = product_nt(grad_inner, w_up)
    grad_input, grad_gain = normalize_back(grad_entry, normal_rows, inverse_deviation, gain)
    return (grad_state + grad_input, (grad_gain, grad_up, grad_down))


def block_scores(query, keys, segment, valid_frames, row_start, block_rows):
    scores = jnp.einsum("qhd,khd->hqk", query, keys, preferred_element_type=jnp.float32)
    row_ids = jnp.arange(block_rows, dtype=jnp.int32) + row_start
    col_ids = jnp.arange(keys.shape[0], dtype=jnp.int32)
    allowed = (segment[row_start : row_start + block_rows, None] == segment[None, :]) & (
        (valid_frames[None, :] > 0) | (row_ids[:, None] == col_ids[None, :])
    )
    return jnp.where(allowed[None, :, :], scores, -1000000000.0)


def attention(values, gain, w_joint, w_out, segment, position, valid_frames):
    normed, normal_rows, inverse_deviation = normalize(values, gain)
    entry_value = normed.astype(jnp.bfloat16)
    slots = values.shape[0]
    joint_projection = product(entry_value, w_joint).reshape(slots, 3, HEADS, HDIM)
    query = (rotate(joint_projection[:, 0], position, 1.0) * HDIM ** (-0.5)).astype(jnp.bfloat16)
    keys = rotate(joint_projection[:, 1], position, 1.0).astype(jnp.bfloat16)
    vals = joint_projection[:, 2].astype(jnp.bfloat16)
    block_rows = min(512, slots)
    scores = block_scores(query, keys, segment, valid_frames, 0, block_rows)
    row_max = jnp.max(scores, axis=-1, keepdims=True)
    expo = jnp.exp(scores - row_max)
    row_sum = jnp.sum(expo, axis=-1, keepdims=True)
    probs = (expo / row_sum).astype(jnp.bfloat16)
    outputs = jnp.einsum("hqk,khd->qhd", probs, vals, preferred_element_type=jnp.float32).astype(
        jnp.bfloat16
    )
    totals = row_max + jnp.log(row_sum)
    mixed_rows = outputs.reshape(slots, HEADS * HDIM)
    return (
        product(mixed_rows, w_out),
        (entry_value, normal_rows, inverse_deviation, query, keys, vals, totals, mixed_rows),
    )


def attend_back(grad_state, gain, w_joint, w_out, segment, position, valid_frames, saved_tensors):
    entry_value, normal_rows, inverse_deviation, query, keys, vals, log_total, mixed_rows = (
        saved_tensors
    )
    slots = grad_state.shape[0]
    grad_branch = grad_state.astype(jnp.bfloat16)
    grad_out = product_tn(mixed_rows, grad_branch)
    grad_mixed = product_nt(grad_branch, w_out).astype(jnp.bfloat16).reshape(slots, HEADS, HDIM)
    block_rows = min(512, slots)
    scores = block_scores(query, keys, segment, valid_frames, 0, block_rows)
    probs = jnp.exp(scores - log_total)
    grad_probs = jnp.einsum("qhd,khd->hqk", grad_mixed, vals, preferred_element_type=jnp.float32)
    grad_scores = (
        probs * (grad_probs - jnp.sum(probs * grad_probs, axis=-1, keepdims=True))
    ).astype(jnp.bfloat16)
    query_parts = jnp.einsum("hqk,khd->qhd", grad_scores, keys, preferred_element_type=jnp.float32)
    grad_keys = jnp.einsum("hqk,qhd->khd", grad_scores, query, preferred_element_type=jnp.float32)
    grad_vals = jnp.einsum(
        "hqk,qhd->khd", probs.astype(jnp.bfloat16), grad_mixed, preferred_element_type=jnp.float32
    )
    grad_query = rotate(query_parts * HDIM ** (-0.5), position, -1.0)
    grad_keys = rotate(grad_keys, position, -1.0)
    grad_joint = jnp.stack([grad_query, grad_keys, grad_vals], axis=1).reshape(
        slots, 3 * HEADS * HDIM
    )
    grad_joint = grad_joint.astype(jnp.bfloat16)
    grad_w_joint = product_tn(entry_value, grad_joint)
    grad_entry = product_nt(grad_joint, w_joint)
    grad_input, grad_gain = normalize_back(grad_entry, normal_rows, inverse_deviation, gain)
    return (grad_state + grad_input, (grad_gain, grad_w_joint, grad_out))


def conv_forward(
    values, gain, w_in, kernel, batch_gain_part, batch_bias_part, w_out, segment, valid_frames
):
    normed, normal_rows, inverse_deviation = normalize(values, gain)
    entry_value = normed.astype(jnp.bfloat16)
    joint_projection = product(entry_value, w_in)
    width = joint_projection.shape[1] // 2
    gate_sigmoid = jax.nn.sigmoid(joint_projection[:, width:])
    gated_linear_unit = joint_projection[:, :width] * gate_sigmoid * valid_frames[:, None]
    mixed_rows = jnp.zeros(gated_linear_unit.shape, jnp.float32)
    for offset in range(KER):
        shift_by = offset - (KER - 1) // 2
        same = (shifted(segment, shift_by, -1) == segment).astype(jnp.float32)[:, None]
        mixed_rows = mixed_rows + kernel[offset] * shifted(gated_linear_unit, shift_by, 0.0) * same
    local_sums = (
        jnp.sum(mixed_rows * valid_frames[:, None], axis=0),
        jnp.sum(mixed_rows * mixed_rows * valid_frames[:, None], axis=0),
        jnp.sum(valid_frames),
    )
    sum_first, sum_second, frame_count = lax.psum(
        (local_sums[0], local_sums[1], local_sums[2]), ("dp", "fsdp")
    )
    centered_rows = sum_first / frame_count
    batch_inverse_std = lax.rsqrt(sum_second / frame_count - centered_rows * centered_rows + EPS)
    normalized_input = (mixed_rows - centered_rows) * batch_inverse_std
    batch_normed_rows = normalized_input * batch_gain_part + batch_bias_part
    activation_value = (batch_normed_rows * jax.nn.sigmoid(batch_normed_rows)).astype(jnp.bfloat16)
    saved_tensors = (
        entry_value,
        normal_rows,
        inverse_deviation,
        joint_projection,
        gate_sigmoid,
        gated_linear_unit,
        normalized_input,
        batch_inverse_std,
        batch_normed_rows,
        activation_value,
        frame_count,
    )
    return (product(activation_value, w_out), saved_tensors)


def conv_back(
    grad_state, gain, w_in, kernel, batch_gain_part, w_out, segment, valid_frames, saved_tensors
):
    (
        entry_value,
        normal_rows,
        inverse_deviation,
        joint_projection,
        gate_sigmoid,
        gated_linear_unit,
        normalized_input,
        batch_inverse_std,
        batch_normed_rows,
        activation_value,
        frame_count,
    ) = saved_tensors
    grad_branch = grad_state.astype(jnp.bfloat16)
    grad_w_out = product_tn(activation_value, grad_branch)
    batch_gradient = product_nt(grad_branch, w_out) * swish_grad(batch_normed_rows)
    local_bias = jnp.sum(batch_gradient, axis=0)
    local_gain_sum = jnp.sum(batch_gradient * normalized_input, axis=0)
    summed_bias_gradient, summed_gain_gradient = lax.psum(
        (local_bias, local_gain_sum), ("dp", "fsdp")
    )
    grad_mixed = batch_inverse_std * (
        batch_gradient * batch_gain_part
        - valid_frames[:, None]
        / frame_count
        * (
            batch_gain_part * summed_bias_gradient
            + normalized_input * batch_gain_part * summed_gain_gradient
        )
    )
    grad_glu = jnp.zeros(gated_linear_unit.shape, jnp.float32)
    kernel_rows = []
    for offset in range(KER):
        shift_by = offset - (KER - 1) // 2
        same_fwd = (shifted(segment, shift_by, -1) == segment).astype(jnp.float32)[:, None]
        kernel_rows.append(
            jnp.sum(grad_mixed * shifted(gated_linear_unit, shift_by, 0.0) * same_fwd, axis=0)
        )
        same_back = (shifted(segment, -shift_by, -1) == segment).astype(jnp.float32)[:, None]
        grad_glu = grad_glu + kernel[offset] * shifted(grad_mixed, -shift_by, 0.0) * same_back
    grad_glu = grad_glu * valid_frames[:, None]
    width = joint_projection.shape[1] // 2
    grad_joint = jnp.concatenate(
        [
            grad_glu * gate_sigmoid,
            grad_glu * joint_projection[:, :width] * gate_sigmoid * (1.0 - gate_sigmoid),
        ],
        axis=1,
    )
    grad_joint = grad_joint.astype(jnp.bfloat16)
    grad_w_in = product_tn(entry_value, grad_joint)
    grad_entry = product_nt(grad_joint, w_in)
    grad_input, grad_gain = normalize_back(grad_entry, normal_rows, inverse_deviation, gain)
    grads = (grad_gain, grad_w_in, jnp.stack(kernel_rows), local_gain_sum, local_bias, grad_w_out)
    return (grad_state + grad_input, grads)


def collect(shards):
    return (
        lax.all_gather(shards[0], "fsdp", axis=0, tiled=True),
        lax.all_gather(shards[1], "fsdp", axis=0, tiled=True),
        lax.all_gather(shards[2], "fsdp", axis=0, tiled=True),
        lax.all_gather(shards[3], "fsdp", axis=0, tiled=True),
        lax.all_gather(shards[4], "fsdp", axis=0, tiled=True),
        lax.all_gather(shards[5], "fsdp", axis=0, tiled=True),
        lax.all_gather(shards[6], "fsdp", axis=0, tiled=True),
        lax.all_gather(shards[7], "fsdp", axis=0, tiled=True),
        lax.all_gather(shards[8], "fsdp", axis=0, tiled=True),
        lax.all_gather(shards[9], "fsdp", axis=0, tiled=True),
        lax.all_gather(shards[10], "fsdp", axis=0, tiled=True),
        lax.all_gather(shards[11], "fsdp", axis=0, tiled=True),
        lax.all_gather(shards[12], "fsdp", axis=0, tiled=True),
        lax.all_gather(shards[13], "fsdp", axis=0, tiled=True),
        lax.all_gather(shards[14], "fsdp", axis=0, tiled=True),
        lax.all_gather(shards[15], "fsdp", axis=0, tiled=True),
    )


def add_tuples(first_set, second_set):
    return tuple((left_item + right_item for left_item, right_item in zip(first_set, second_set)))


def body(
    frames,
    item_lengths,
    frame_mask,
    first_norm,
    first_up,
    first_down,
    attend_norm,
    attend_joint,
    attend_out,
    conv_norm,
    conv_in,
    conv_kernel,
    batch_gain,
    batch_bias,
    conv_out,
    second_norm,
    second_up,
    second_down,
    final_norm,
    output_grad,
):
    shards = (
        first_norm,
        first_up,
        first_down,
        attend_norm,
        attend_joint,
        attend_out,
        conv_norm,
        conv_in,
        conv_kernel,
        batch_gain,
        batch_bias,
        conv_out,
        second_norm,
        second_up,
        second_down,
        final_norm,
    )
    slots = frames.shape[1]
    parts = None
    outputs = []
    input_grads = []
    for micro in range(MB):
        full = collect(shards)
        (
            norm_one,
            up_one,
            down_one,
            norm_attend,
            joint_attend,
            out_attend,
            norm_conv,
            in_conv,
            kernel_conv,
            batch_gain_part,
            batch_bias_part,
            out_conv,
            norm_two,
            up_two,
            down_two,
            norm_last,
        ) = full
        segment, position = frame_layout(item_lengths[micro, 0], slots)
        valid_frames = frame_mask[micro].astype(jnp.float32)
        entered = frames[micro].astype(jnp.float32)
        branch, saved_one = feed_forward(entered, norm_one.astype(jnp.float32), up_one, down_one)
        after_one = entered + 0.5 * branch
        branch, saved_attend = attention(
            after_one,
            norm_attend.astype(jnp.float32),
            joint_attend,
            out_attend,
            segment,
            position,
            valid_frames,
        )
        after_attend = after_one + branch
        branch, saved_conv = conv_forward(
            after_attend,
            norm_conv.astype(jnp.float32),
            in_conv,
            kernel_conv.astype(jnp.float32),
            batch_gain_part.astype(jnp.float32),
            batch_bias_part.astype(jnp.float32),
            out_conv,
            segment,
            valid_frames,
        )
        after_conv = after_attend + branch
        branch, saved_two = feed_forward(after_conv, norm_two.astype(jnp.float32), up_two, down_two)
        after_two = after_conv + 0.5 * branch
        final_out, final_normal, final_inv = normalize(after_two, norm_last.astype(jnp.float32))
        outputs.append(final_out.astype(jnp.bfloat16))
        back_full = (
            lax.all_gather(shards[0], "fsdp", axis=0, tiled=True),
            lax.all_gather(shards[1], "fsdp", axis=0, tiled=True),
            lax.all_gather(shards[2], "fsdp", axis=0, tiled=True),
            lax.all_gather(shards[3], "fsdp", axis=0, tiled=True),
            lax.all_gather(shards[4], "fsdp", axis=0, tiled=True),
            lax.all_gather(shards[5], "fsdp", axis=0, tiled=True),
            lax.all_gather(shards[6], "fsdp", axis=0, tiled=True),
            lax.all_gather(shards[7], "fsdp", axis=0, tiled=True),
            lax.all_gather(shards[8], "fsdp", axis=0, tiled=True),
            lax.all_gather(shards[9], "fsdp", axis=0, tiled=True),
            lax.all_gather(shards[10], "fsdp", axis=0, tiled=True),
            lax.all_gather(shards[11], "fsdp", axis=0, tiled=True),
            lax.all_gather(shards[12], "fsdp", axis=0, tiled=True),
            lax.all_gather(shards[13], "fsdp", axis=0, tiled=True),
            lax.all_gather(shards[14], "fsdp", axis=0, tiled=True),
            lax.all_gather(shards[15], "fsdp", axis=0, tiled=True),
        )
        (
            norm_one,
            up_one,
            down_one,
            norm_attend,
            joint_attend,
            out_attend,
            norm_conv,
            in_conv,
            kernel_conv,
            batch_gain_part,
            batch_bias_part,
            out_conv,
            norm_two,
            up_two,
            down_two,
            norm_last,
        ) = back_full
        grad_state, grad_last = normalize_back(
            output_grad[micro].astype(jnp.float32),
            final_normal,
            final_inv,
            norm_last.astype(jnp.float32),
        )
        grad_state, grads_two = feed_back(
            grad_state, norm_two.astype(jnp.float32), up_two, down_two, saved_two
        )
        grad_state, grads_conv = conv_back(
            grad_state,
            norm_conv.astype(jnp.float32),
            in_conv,
            kernel_conv.astype(jnp.float32),
            batch_gain_part.astype(jnp.float32),
            out_conv,
            segment,
            valid_frames,
            saved_conv,
        )
        grad_state, grads_attend = attend_back(
            grad_state,
            norm_attend.astype(jnp.float32),
            joint_attend,
            out_attend,
            segment,
            position,
            valid_frames,
            saved_attend,
        )
        grad_state, grads_one = feed_back(
            grad_state, norm_one.astype(jnp.float32), up_one, down_one, saved_one
        )
        input_grads.append(grad_state.astype(jnp.bfloat16))
        grads = (
            grads_one[0],
            grads_one[1],
            grads_one[2],
            grads_attend[0],
            grads_attend[1],
            grads_attend[2],
            grads_conv[0],
            grads_conv[1],
            grads_conv[2],
            grads_conv[3],
            grads_conv[4],
            grads_conv[5],
            grads_two[0],
            grads_two[1],
            grads_two[2],
            grad_last,
        )
        piece = (
            lax.psum_scatter(
                grads[0].astype(jnp.bfloat16), "fsdp", scatter_dimension=0, tiled=True
            ).astype(jnp.float32),
            lax.psum_scatter(
                grads[1].astype(jnp.bfloat16), "fsdp", scatter_dimension=0, tiled=True
            ).astype(jnp.float32),
            lax.psum_scatter(
                grads[2].astype(jnp.bfloat16), "fsdp", scatter_dimension=0, tiled=True
            ).astype(jnp.float32),
            lax.psum_scatter(
                grads[3].astype(jnp.bfloat16), "fsdp", scatter_dimension=0, tiled=True
            ).astype(jnp.float32),
            lax.psum_scatter(
                grads[4].astype(jnp.bfloat16), "fsdp", scatter_dimension=0, tiled=True
            ).astype(jnp.float32),
            lax.psum_scatter(
                grads[5].astype(jnp.bfloat16), "fsdp", scatter_dimension=0, tiled=True
            ).astype(jnp.float32),
            lax.psum_scatter(
                grads[6].astype(jnp.bfloat16), "fsdp", scatter_dimension=0, tiled=True
            ).astype(jnp.float32),
            lax.psum_scatter(
                grads[7].astype(jnp.bfloat16), "fsdp", scatter_dimension=0, tiled=True
            ).astype(jnp.float32),
            lax.psum_scatter(
                grads[8].astype(jnp.bfloat16), "fsdp", scatter_dimension=0, tiled=True
            ).astype(jnp.float32),
            lax.psum_scatter(
                grads[9].astype(jnp.bfloat16), "fsdp", scatter_dimension=0, tiled=True
            ).astype(jnp.float32),
            lax.psum_scatter(
                grads[10].astype(jnp.bfloat16), "fsdp", scatter_dimension=0, tiled=True
            ).astype(jnp.float32),
            lax.psum_scatter(
                grads[11].astype(jnp.bfloat16), "fsdp", scatter_dimension=0, tiled=True
            ).astype(jnp.float32),
            lax.psum_scatter(
                grads[12].astype(jnp.bfloat16), "fsdp", scatter_dimension=0, tiled=True
            ).astype(jnp.float32),
            lax.psum_scatter(
                grads[13].astype(jnp.bfloat16), "fsdp", scatter_dimension=0, tiled=True
            ).astype(jnp.float32),
            lax.psum_scatter(
                grads[14].astype(jnp.bfloat16), "fsdp", scatter_dimension=0, tiled=True
            ).astype(jnp.float32),
            lax.psum_scatter(
                grads[15].astype(jnp.bfloat16), "fsdp", scatter_dimension=0, tiled=True
            ).astype(jnp.float32),
        )
        parts = piece if parts is None else add_tuples(parts, piece)
    totals = lax.psum(parts, "dp")
    return (
        jnp.stack(outputs),
        jnp.stack(input_grads),
        totals[0],
        totals[1],
        totals[2],
        totals[3],
        totals[4],
        totals[5],
        totals[6],
        totals[7],
        totals[8],
        totals[9],
        totals[10],
        totals[11],
        totals[12],
        totals[13],
        totals[14],
        totals[15],
    )


def solution(mesh):
    return jax.shard_map(
        body,
        mesh=mesh,
        in_specs=(
            P(None, ("dp", "fsdp"), None),
            P(None, ("dp", "fsdp"), None),
            P(None, ("dp", "fsdp")),
            P("fsdp"),
            P("fsdp", None),
            P("fsdp", None),
            P("fsdp"),
            P("fsdp", None),
            P("fsdp", None),
            P("fsdp"),
            P("fsdp", None),
            P("fsdp", None),
            P("fsdp"),
            P("fsdp"),
            P("fsdp", None),
            P("fsdp"),
            P("fsdp", None),
            P("fsdp", None),
            P("fsdp"),
            P(None, ("dp", "fsdp"), None),
        ),
        out_specs=(
            P(None, ("dp", "fsdp"), None),
            P(None, ("dp", "fsdp"), None),
            P("fsdp"),
            P("fsdp", None),
            P("fsdp", None),
            P("fsdp"),
            P("fsdp", None),
            P("fsdp", None),
            P("fsdp"),
            P("fsdp", None),
            P("fsdp", None),
            P("fsdp"),
            P("fsdp"),
            P("fsdp", None),
            P("fsdp"),
            P("fsdp", None),
            P("fsdp", None),
            P("fsdp"),
        ),
        check_vma=False,
    )
```

profile of v0, /device:TPU:0, one launch (start us, length us, event | category | flops | bytes accessed | tf_op | source)
XLA Modules:
  0.0 1034.7 jit_solution(18431604311222931992)
XLA Ops:
  14.1 5.3 all_gather.38
  24.4 4.4 all-gather
  29.9 4.4 all-gather.1
  35.5 14.4 %all_gather.37 = bf16[512,512]{1,0:T(8,128)(2,1)} all-gather(bf16[256,512]{1,0:T(8,128)(2,1)S(1)} %copy-done.116), channel_id=1, replica_groups=mesh['dp'=16,'fsdp'=2] {'fsdp'}, dimensions={0}, use_global_device_ids=true | all-gather | bytes 786432 | tf_op jit(solution)/shard_map/all_gather | solution.py:282
  50.0 4.2 all-gather.2
  54.8 4.2 all-gather.3
  59.6 4.2 all-gather.4
  64.4 12.9 %all_gather.43 = bf16[512,512]{1,0:T(8,128)(2,1)} all-gather(bf16[256,512]{1,0:T(8,128)(2,1)S(1)} %copy-done.117), channel_id=1, replica_groups=mesh['dp'=16,'fsdp'=2] {'fsdp'}, dimensions={0}, use_global_device_ids=true | all-gather | bytes 786432 | tf_op jit(solution)/shard_map/all_gather | solution.py:288
  77.3 4.4 all-gather.5
  82.3 4.4 all-gather.6
  92.1 6.2 multiply_convert_fusion.9
  98.3 4.0 fusion.495
  102.4 3.9 multiply_convert_fusion.7
  108.1 11.4 %all-gather.18.cloned.1.call-done = bf16[512,1536]{1,0:T(8,128)(2,1)} async-done(((bf16[256,1536]{1,0:T(8,128)(2,1)}), bf16[512,1536]{1,0:T(8,128)(2,1)}) %all-gather.18.cloned.1.call-update) | async-done | bytes 1572880 | tf_op jit(solution)/shard_map/all_gather | solution.py:281
  150.8 9.3 multiply_reduce_fusion.89
  160.2 9.0 multiply_reduce_fusion.83
  169.1 40.4 %all-reduce.21 = (f32[512]{0:T(512)}, f32[]{:T(128)}, f32[512]{0:T(512)}, f32[512]{0:T(512)}, f32[]{:T(128)}, /*index=5*/f32[512]{0:T(512)}) all-reduce(f32[512]{0:T(512)} %get-tuple-element.185, f32[]{:T(128)} %get-tuple-element.193, f32[512]{0:T(512)} %get-tuple-element.184, ...), channel_id=1, replica_groups=mesh['dp'=16,'fsdp'=2] {'dp','fsdp'}, use_global_device_ids=true, to_apply=%region_37.38 | all-reduce | flops 2050 | bytes 16400 | tf_op jit(solution)/shard_map/psum | solution.py:191
  215.1 5.3 fusion.476
  220.4 4.7 fusion.499
  234.9 2.8 multiply_convert_fusion.5
  244.9 4.1 fusion.484
  251.5 5.7 multiply_convert_fusion.3
  263.7 42.3 %all-reduce.20 = (f32[512]{0:T(512)}, f32[512]{0:T(512)}, f32[512]{0:T(512)}, f32[512]{0:T(512)}) all-reduce(f32[512]{0:T(512)} %get-tuple-element.189, f32[512]{0:T(512)} %get-tuple-element.188, f32[512]{0:T(512)} %get-tuple-element.187, f32[512]{0:T(512)} %get-tuple-element.186), channel_id=1, replica_groups=mesh['dp'=16,'fsdp'=2] {'dp','fsdp'}, use_global_device_ids=true, to_apply=%region_64.65 | all-reduce | flops 2048 | bytes 16384 | tf_op jit(solution)/shard_map/psum | solution.py:236
  307.6 5.0 multiply_reduce_fusion.36
  313.0 7.7 multiply_convert_fusion.16
  328.1 5.0 multiply_reduce_fusion.4
  333.5 8.2 multiply_convert_fusion.12
  343.8 2.7 multiply_reduce_fusion.68
  356.6 2.6 convolution_convert_fusion.13
  361.0 3.3 convolution_convert_fusion.10
  364.4 6.5 multiply_reduce_fusion.1
  370.9 2.6 multiply_convert_fusion.1
  379.9 5.4 fusion.53
  390.4 6.5 multiply_reduce_fusion
  396.9 2.6 multiply_convert_fusion
  408.7 6.0 convolution_convert_fusion.3
  415.4 5.9 convolution_convert_fusion.2
  421.9 4.6 convolution_convert_fusion.5
  427.2 4.6 convolution_convert_fusion.4
  431.9 3.8 multiply_reduce_fusion.71
  442.7 2.6 convolution_convert_fusion.9
  447.7 4.4 multiply_convert_fusion.2
  453.4 2.6 convolution_convert_fusion.8
  457.3 4.2 convolution_convert_fusion.7
  463.0 4.3 convolution_convert_fusion.6
  491.1 2.7 convert_add_fusion.4
  493.8 22.6 %reduce-scatter.51.cloned.1.call-done = bf16[1024,512]{1,0:T(8,128)(2,1)} async-done(((bf16[2048,512]{1,0:T(8,128)(2,1)}), bf16[1024,512]{1,0:T(8,128)(2,1)}) %reduce-scatter.51.cloned.1.call-update) | async-done | bytes 1048592 | tf_op jit(solution)/shard_map/reduce_scatter | solution.py:526
  516.4 34.0 %reduce-scatter.53.cloned.1.call-done = bf16[1024,512]{1,0:T(8,128)(2,1)} async-done(((bf16[2048,512]{1,0:T(8,128)(2,1)}), bf16[1024,512]{1,0:T(8,128)(2,1)}) %reduce-scatter.53.cloned.1.call-update) | async-done | bytes 1048592 | tf_op jit(solution)/shard_map/reduce_scatter | solution.py:526
  550.5 3.2 convert_add_fusion
  553.7 30.8 %reduce-scatter.47.cloned.1.call-done = bf16[256,2048]{1,0:T(8,128)(2,1)} async-done(((bf16[512,2048]{1,0:T(8,128)(2,1)}), bf16[256,2048]{1,0:T(8,128)(2,1)}) %reduce-scatter.47.cloned.1.call-update) | async-done | bytes 1048592 | tf_op jit(solution)/shard_map/reduce_scatter | solution.py:523
  584.5 34.0 %reduce-scatter.49.cloned.1.call-done = bf16[256,2048]{1,0:T(8,128)(2,1)} async-done(((bf16[512,2048]{1,0:T(8,128)(2,1)}), bf16[256,2048]{1,0:T(8,128)(2,1)}) %reduce-scatter.49.cloned.1.call-update) | async-done | bytes 1048592 | tf_op jit(solution)/shard_map/reduce_scatter | solution.py:523
  618.5 3.2 convert_add_fusion.1
  621.7 31.0 %reduce-scatter.19.cloned.1.call-done = bf16[256,2048]{1,0:T(8,128)(2,1)} async-done(((bf16[512,2048]{1,0:T(8,128)(2,1)}), bf16[256,2048]{1,0:T(8,128)(2,1)}) %reduce-scatter.19.cloned.1.call-update) | async-done | bytes 1048592 | tf_op jit(solution)/shard_map/reduce_scatter | solution.py:487
  652.7 34.6 %reduce-scatter.21.cloned.1.call-done = bf16[256,2048]{1,0:T(8,128)(2,1)} async-done(((bf16[512,2048]{1,0:T(8,128)(2,1)}), bf16[256,2048]{1,0:T(8,128)(2,1)}) %reduce-scatter.21.cloned.1.call-update) | async-done | bytes 1048592 | tf_op jit(solution)/shard_map/reduce_scatter | solution.py:487
  687.3 3.2 convert_add_fusion.3
  690.5 31.0 %reduce-scatter.23.cloned.1.call-done = bf16[1024,512]{1,0:T(8,128)(2,1)} async-done(((bf16[2048,512]{1,0:T(8,128)(2,1)}), bf16[1024,512]{1,0:T(8,128)(2,1)}) %reduce-scatter.23.cloned.1.call-update) | async-done | bytes 1048592 | tf_op jit(solution)/shard_map/reduce_scatter | solution.py:490
  721.5 34.2 %reduce-scatter.25.cloned.1.call-done = bf16[1024,512]{1,0:T(8,128)(2,1)} async-done(((bf16[2048,512]{1,0:T(8,128)(2,1)}), bf16[1024,512]{1,0:T(8,128)(2,1)}) %reduce-scatter.25.cloned.1.call-update) | async-done | bytes 1048592 | tf_op jit(solution)/shard_map/reduce_scatter | solution.py:490
  755.7 3.2 convert_add_fusion.2
  760.9 3.3 fusion.258
  770.1 7.0 all-reduce.24
  777.7 2.8 reduce-scatter.41.cloned.1.call-done
  781.2 64.0 %all-reduce.22 = (f32[256]{0:T(256)}, f32[256]{0:T(256)}, f32[256]{0:T(256)}, f32[16,512]{1,0:T(8,128)}, f32[256]{0:T(256)}, /*index=5*/f32[256]{0:T(256)}, f32[256]{0:T(256)}, f32[256]{0:T(256)}) all-reduce(f32[256]{0:T(256)S(1)} %convert_add_fusion.15, f32[256]{0:T(256)S(1)} %convert_add_fusion.14, ...), channel_id=1, replica_groups=mesh['dp'=16,'fsdp'=2] {'dp'}, use_global_device_ids=true, to_apply=%region_76.77 | all-reduce | flops 9984 | bytes 79872 | tf_op jit(solution)/shard_map/psum | solution.py:534
  845.2 169.7 %all-reduce.27.cloned.1.call-done = (f32[256,2048]{1,0:T(8,128)}, f32[1024,512]{1,0:T(8,128)}, f32[256,1536]{1,0:T(8,128)}, f32[256,512]{1,0:T(8,128)}, f32[256,...) async-done(((f32[256,2048]{1,0:T(8,128)}, f32[1024,512]{1,0:T(8,128)}, f32[256,1536]{1,0:T(8,128)}, f32[256,512]{1,0:T(8,128)}, ...) | async-done | bytes 12058640 | tf_op jit(solution)/shard_map/psum | solution.py:534
  1014.9 3.3 copy.126
  (1210 shorter events, 182.6 us)
Async XLA Ops:
  7.2 84.9 %all-gather.14.cloned.1.call-start = ((), (), s32[]{:S(2)}) async-start(), calls=%async_computation.18 | async-start | bytes 3145728 | tf_op jit(solution)/shard_map/all_gather | solution.py:278
  8.0 90.4 %all-gather.16.cloned.1.call-start = ((), (), s32[]{:S(2)}) async-start(), calls=%async_computation.19 | async-start | bytes 3145728 | tf_op jit(solution)/shard_map/all_gather | solution.py:279
  8.7 14.4 %copy-start.105 = (bf16[2,512,512]{2,1,0:T(8,128)(2,1)S(1)}, bf16[2,512,512]{2,1,0:T(8,128)(2,1)}, u32[]{:S(2)}) copy-start(bf16[2,512,512]{2,1,0:T(8,128)(2,1)} %param.20) | copy-start | bytes 3145732
  8.7 110.8 %all-gather.18.cloned.1.call-start = ((), (), s32[]{:S(2)}) async-start(), calls=%async_computation.20 | async-start | bytes 2359296 | tf_op jit(solution)/shard_map/all_gather | solution.py:281
  9.4 134.4 %all-gather.20.cloned.1.call-start = ((), (), s32[]{:S(2)}) async-start(), calls=%async_computation.21 | async-start | bytes 1572864 | tf_op jit(solution)/shard_map/all_gather | solution.py:284
  10.0 205.1 %all-gather.22.cloned.1.call-start = ((), (), s32[]{:S(2)}) async-start(), calls=%async_computation.22 | async-start | bytes 3145728 | tf_op jit(solution)/shard_map/all_gather | solution.py:290
  10.6 209.8 %all-gather.24.cloned.1.call-start = ((), (), s32[]{:S(2)}) async-start(), calls=%async_computation.23 | async-start | bytes 3145728 | tf_op jit(solution)/shard_map/all_gather | solution.py:291
  11.2 473.6 %reduce-scatter.43.cloned.1.call-start = ((), (), s32[]{:S(2)}) async-start(), calls=%async_computation.36 | async-start | bytes 786432 | tf_op jit(solution)/shard_map/reduce_scatter | solution.py:517
  23.2 12.3 %copy-start.116 = (bf16[256,512]{1,0:T(8,128)(2,1)S(1)}, bf16[256,512]{1,0:T(8,128)(2,1)}, u32[]{:S(2)}) copy-start(bf16[256,512]{1,0:T(8,128)(2,1)} %param.28) | copy-start | bytes 786436
  23.4 74.9 %copy-start.46 = (bf16[1,512,512]{1,2,0:T(8,128)(2,1)}, bf16[1,512,512]{1,2,0:T(8,128)(2,1)S(1)}, u32[]{:S(2)}) copy-start(bf16[1,512,512]{1,2,0:T(8,128)(2,1)S(1)} %copy.114) | copy-start | bytes 1572868
  23.4 26.5 %copy-start.426 = (bf16[256]{0:T(256)(128)(2,1)S(1)}, bf16[256]{0:T(256)(128)(2,1)}, u32[]{:S(2)}) copy-start(bf16[256]{0:T(256)(128)(2,1)} %param.29) | copy-start | bytes 1540
  23.4 31.4 %copy-start.427 = (bf16[256]{0:T(256)(128)(2,1)S(1)}, bf16[256]{0:T(256)(128)(2,1)}, u32[]{:S(2)}) copy-start(bf16[256]{0:T(256)(128)(2,1)} %param.32) | copy-start | bytes 1540
  23.5 36.2 %copy-start.428 = (bf16[256]{0:T(256)(128)(2,1)S(1)}, bf16[256]{0:T(256)(128)(2,1)}, u32[]{:S(2)}) copy-start(bf16[256]{0:T(256)(128)(2,1)} %param.33) | copy-start | bytes 1540
  23.5 41.0 %copy-start.117 = (bf16[256,512]{1,0:T(8,128)(2,1)S(1)}, bf16[256,512]{1,0:T(8,128)(2,1)}, u32[]{:S(2)}) copy-start(bf16[256,512]{1,0:T(8,128)(2,1)} %param.34) | copy-start | bytes 786436
  23.6 68.5 %copy-start.342 = (f32[512]{0:T(512)}, f32[512]{0:T(512)S(1)}, u32[]{:S(2)}) copy-start(f32[512]{0:T(512)S(1)} %broadcast_multiply_fusion.31) | copy-start | bytes 6148
  23.6 53.7 %copy-start.429 = (bf16[256]{0:T(256)(128)(2,1)S(1)}, bf16[256]{0:T(256)(128)(2,1)}, u32[]{:S(2)}) copy-start(bf16[256]{0:T(256)(128)(2,1)} %param.35) | copy-start | bytes 1540
  23.6 58.7 %copy-start.430 = (bf16[256]{0:T(256)(128)(2,1)S(1)}, bf16[256]{0:T(256)(128)(2,1)}, u32[]{:S(2)}) copy-start(bf16[256]{0:T(256)(128)(2,1)} %param.38) | copy-start | bytes 1540
  23.6 63.6 %copy-start.106 = (bf16[2,512,512]{2,1,0:T(8,128)(2,1)S(1)}, bf16[2,512,512]{2,1,0:T(8,128)(2,1)}, u32[]{:S(2)}) copy-start(bf16[2,512,512]{2,1,0:T(8,128)(2,1)} %param.39) | copy-start | bytes 3145732
  28.8 73.5 %copy-start.349 = (f32[2,1,256]{2,1,0:T(1,128)}, f32[2,1,256]{2,1,0:T(1,128)S(1)}, u32[]{:S(2)}) copy-start(f32[2,1,256]{2,1,0:T(1,128)S(1)} %convert_element_type.988) | copy-start | bytes 6148
  29.0 77.3 %copy-start.29 = (bf16[1,512,512]{1,2,0:T(8,128)(2,1)}, bf16[1,512,512]{1,2,0:T(8,128)(2,1)S(1)}, u32[]{:S(2)}) copy-start(bf16[1,512,512]{1,2,0:T(8,128)(2,1)S(1)} %copy.115) | copy-start | bytes 1572868
  29.2 73.2 %copy-start.272 = (f32[512]{0:T(512)}, f32[512]{0:T(512)S(1)}, u32[]{:S(2)}) copy-start(f32[512]{0:T(512)S(1)} %broadcast_multiply_fusion.26) | copy-start | bytes 6148
  34.3 97.9 %copy-start.126 = (f32[2,1,256]{2,1,0:T(1,128)}, f32[2,1,256]{2,1,0:T(1,128)S(1)}, u32[]{:S(2)}) copy-start(f32[2,1,256]{2,1,0:T(1,128)S(1)} %convert_element_type.989) | copy-start | bytes 6148
  102.3 28.5 %copy-start.14 = (f32[512,512]{0,1:T(8,128)}, f32[512,512]{0,1:T(8,128)S(1)}, u32[]{:S(2)}) copy-start(f32[512,512]{0,1:T(8,128)S(1)} %get-tuple-element.414) | copy-start | bytes 3145732
  102.4 17.2 %copy-start.137 = (f32[512]{0:T(512)}, f32[512]{0:T(512)S(1)}, u32[]{:S(2)}) copy-start(f32[512]{0:T(512)S(1)} %broadcast_multiply_fusion.30) | copy-start | bytes 6148
  107.7 24.5 %copy-start.124 = (f32[512]{0:T(512)}, f32[512]{0:T(512)S(1)}, u32[]{:S(2)}) copy-start(f32[512]{0:T(512)S(1)} %broadcast_multiply_fusion.25) | copy-start | bytes 6148
  108.1 14.0 %copy-start.146 = (f32[512]{0:T(512)}, f32[512]{0:T(512)S(1)}, u32[]{:S(2)}) copy-start(f32[512]{0:T(512)S(1)} %get-tuple-element.445) | copy-start | bytes 6148
  108.1 24.1 %copy-start.139 = (f32[512]{0:T(512)}, f32[512]{0:T(512)S(1)}, u32[]{:S(2)}) copy-start(f32[512]{0:T(512)S(1)} %get-tuple-element.444) | copy-start | bytes 6148
  131.4 12.5 %copy-start.19 = (f32[512,512]{0,1:T(8,128)}, f32[512,512]{0,1:T(8,128)S(1)}, u32[]{:S(2)}) copy-start(f32[512,512]{0,1:T(8,128)S(1)} %get-tuple-element.418) | copy-start | bytes 3145732
  150.1 10.0 copy-start.274
  150.1 10.0 copy-start.276
  150.1 10.0 copy-start.278
  150.1 10.0 copy-start.280
  150.1 10.0 copy-start.282
  150.2 10.0 copy-start.283
  150.2 10.0 copy-start.284
  150.5 9.7 copy-start.285
  225.1 14.8 %copy-start.39 = (f32[512,512]{0,1:T(8,128)}, f32[512,512]{0,1:T(8,128)S(1)}, u32[]{:S(2)}) copy-start(f32[512,512]{0,1:T(8,128)S(1)} %get-tuple-element.424) | copy-start | bytes 3145732
  225.2 14.7 %copy-start.267 = (f32[512]{0:T(512)}, f32[512]{0:T(512)S(1)}, u32[]{:S(2)}) copy-start(f32[512]{0:T(512)S(1)} %broadcast_multiply_fusion.27) | copy-start | bytes 6148
  225.4 14.5 %copy-start.344 = (f32[512]{0:T(512)}, f32[512]{0:T(512)S(1)}, u32[]{:S(2)}) copy-start(f32[512]{0:T(512)S(1)} %add_rsqrt_fusion.6) | copy-start | bytes 6148
  226.4 13.5 %copy-start.369 = (f32[512]{0:T(512)}, f32[512]{0:T(512)S(1)}, u32[]{:S(2)}) copy-start(f32[512]{0:T(512)S(1)} %broadcast_multiply_fusion.20) | copy-start | bytes 6148
  226.4 13.5 %copy-start.371 = (f32[512]{0:T(512)}, f32[512]{0:T(512)S(1)}, u32[]{:S(2)}) copy-start(f32[512]{0:T(512)S(1)} %broadcast_multiply_fusion.21) | copy-start | bytes 6148
  233.0 7.0 copy-start.269
  251.4 233.4 %reduce-scatter.45.cloned.1.call-start = ((), (), s32[]{:S(2)}) async-start(), calls=%async_computation.37 | async-start | bytes 786432 | tf_op jit(solution)/shard_map/reduce_scatter | solution.py:517
  312.7 8.6 copy-start.4
  327.7 159.1 %reduce-scatter.31.cloned.1.call-start = ((), (), s32[]{:S(2)}) async-start(), calls=%async_computation.30 | async-start | bytes 786432 | tf_op jit(solution)/shard_map/reduce_scatter | solution.py:499
  333.2 10.1 copy-start.2
  333.5 9.7 copy-start.66
  333.5 9.7 copy-start.104
  348.9 137.9 %reduce-scatter.33.cloned.1.call-start = ((), (), s32[]{:S(2)}) async-start(), calls=%async_computation.31 | async-start | bytes 786432 | tf_op jit(solution)/shard_map/reduce_scatter | solution.py:499
  354.8 133.9 %reduce-scatter.35.cloned.1.call-start = ((), (), s32[]{:S(2)}) async-start(), calls=%async_computation.32 | async-start | bytes 1572864 | tf_op jit(solution)/shard_map/reduce_scatter | solution.py:505
  364.3 124.4 %reduce-scatter.37.cloned.1.call-start = ((), (), s32[]{:S(2)}) async-start(), calls=%async_computation.33 | async-start | bytes 1572864 | tf_op jit(solution)/shard_map/reduce_scatter | solution.py:505
  377.7 113.3 %reduce-scatter.27.cloned.1.call-start = ((), (), s32[]{:S(2)}) async-start(), calls=%async_computation.28 | async-start | bytes 2359296 | tf_op jit(solution)/shard_map/reduce_scatter | solution.py:496
  390.1 100.9 %reduce-scatter.29.cloned.1.call-start = ((), (), s32[]{:S(2)}) async-start(), calls=%async_computation.29 | async-start | bytes 2359296 | tf_op jit(solution)/shard_map/reduce_scatter | solution.py:496
  408.6 107.8 %reduce-scatter.51.cloned.1.call-start = ((), (), s32[]{:S(2)}) async-start(), calls=%async_computation.40 | async-start | bytes 3145728 | tf_op jit(solution)/shard_map/reduce_scatter | solution.py:526
  414.7 135.7 %reduce-scatter.53.cloned.1.call-start = ((), (), s32[]{:S(2)}) async-start(), calls=%async_computation.41 | async-start | bytes 3145728 | tf_op jit(solution)/shard_map/reduce_scatter | solution.py:526
  421.3 163.2 %reduce-scatter.47.cloned.1.call-start = ((), (), s32[]{:S(2)}) async-start(), calls=%async_computation.38 | async-start | bytes 3145728 | tf_op jit(solution)/shard_map/reduce_scatter | solution.py:523
  426.5 192.0 %reduce-scatter.49.cloned.1.call-start = ((), (), s32[]{:S(2)}) async-start(), calls=%async_computation.39 | async-start | bytes 3145728 | tf_op jit(solution)/shard_map/reduce_scatter | solution.py:523
  431.8 220.9 %reduce-scatter.19.cloned.1.call-start = ((), (), s32[]{:S(2)}) async-start(), calls=%async_computation.24 | async-start | bytes 3145728 | tf_op jit(solution)/shard_map/reduce_scatter | solution.py:487
  445.4 241.9 %reduce-scatter.21.cloned.1.call-start = ((), (), s32[]{:S(2)}) async-start(), calls=%async_computation.25 | async-start | bytes 3145728 | tf_op jit(solution)/shard_map/reduce_scatter | solution.py:487
  456.1 265.4 %reduce-scatter.23.cloned.1.call-start = ((), (), s32[]{:S(2)}) async-start(), calls=%async_computation.26 | async-start | bytes 3145728 | tf_op jit(solution)/shard_map/reduce_scatter | solution.py:490
  461.5 294.2 %reduce-scatter.25.cloned.1.call-start = ((), (), s32[]{:S(2)}) async-start(), calls=%async_computation.27 | async-start | bytes 3145728 | tf_op jit(solution)/shard_map/reduce_scatter | solution.py:490
  467.5 310.2 %reduce-scatter.39.cloned.1.call-start = ((), (), s32[]{:S(2)}) async-start(), calls=%async_computation.34 | async-start | bytes 49152 | tf_op jit(solution)/shard_map/reduce_scatter | solution.py:508
  480.3 300.1 %reduce-scatter.41.cloned.1.call-start = ((), (), s32[]{:S(2)}) async-start(), calls=%async_computation.35 | async-start | bytes 49152 | tf_op jit(solution)/shard_map/reduce_scatter | solution.py:508
  484.6 530.3 %all-reduce.27.cloned.1.call-start = ((), (), s32[]{:S(2)}) async-start(), calls=%async_computation.42 | async-start | bytes 24117248 | tf_op jit(solution)/shard_map/psum | solution.py:534
  (404 other events, 1320.4 us)
Sparse Core Ops, SparseCore 0:
  9.5 41.4 all-gather.13
  52.6 37.2 all-gather.15
  91.4 28.0 all-gather.17
  120.9 21.2 all-gather.19
  143.6 33.2 all-gather.21
  178.3 34.1 all-gather.23
  251.5 15.9 reduce-scatter.42
  327.8 14.6 reduce-scatter.44
  349.0 14.7 reduce-scatter.30
  365.8 14.6 reduce-scatter.32
  382.8 20.3 reduce-scatter.34
  405.3 20.3 reduce-scatter.36
  428.0 26.1 reduce-scatter.26
  456.2 26.1 reduce-scatter.28
  484.5 31.8 reduce-scatter.50
  518.5 31.8 reduce-scatter.52
  552.5 31.8 reduce-scatter.46
  586.6 31.8 reduce-scatter.48
  620.8 31.8 reduce-scatter.18
  655.4 31.8 reduce-scatter.20
  689.6 31.8 reduce-scatter.22
  723.7 31.8 reduce-scatter.24
  757.9 9.9 reduce-scatter.38
  770.5 9.9 reduce-scatter.40
  787.7 227.1 all-reduce.26
where the time goes:
time: 1040 us; the launch traced here: 1030 us
  waiting for transfers between devices  440 us (42%)
  blocking collectives  217 us (21%)
  matrix products  168 us (16%)
  other arithmetic  129 us (12%)
  local copies, waits for them, and re-layouts  57.5 us (6%)
  between operations  21.3 us (2%)
    psum x1, waiting for transfers between devices, body(): totals = lax.psum(parts, 'dp')  170 us
    reduce_scatter x2, waiting for transfers between devices, body(): lax.psum_scatter(grads[1].astype(jnp.bfloat16), 'fsdp', scatter_dimension...  65.6 us
    reduce_scatter x2, waiting for transfers between devices, body(): lax.psum_scatter(grads[2].astype(jnp.bfloat16), 'fsdp', scatter_dimension...  65.1 us
    reduce_scatter x2, waiting for transfers between devices, body(): lax.psum_scatter(grads[13].astype(jnp.bfloat16), 'fsdp', scatter_dimensio...  64.9 us
    psum x1, blocking collectives, body(): totals = lax.psum(parts, 'dp')  64 us
    reduce_scatter x2, waiting for transfers between devices, body(): lax.psum_scatter(grads[14].astype(jnp.bfloat16), 'fsdp', scatter_dimensio...  56.7 us
    unnamed x908, local copies, waits for them, and re-layouts  50.3 us
    dot_general x16, matrix products, product_tn(): lax.dot_general(left, right, (((0,), (0,)), ((), ())), preferred_element_...  49.6 us
  transfers between devices with their start and end apart: 25, of which 11 were waited for; matrix products, arithmetic and copies ran while one was open for 27% of the time, Pallas kernels for 0%

commit v1 on v0

--- a/solution.py
+++ b/solution.py
@@ -1,3 +1,4 @@
+import functools
 import math
 
 import jax
@@ -12,6 +13,57 @@
 
 
 EPS = 1e-05
+
+def swap(value, axis, bit, size):
+    return lax.ppermute(value, axis, [(i, i ^ bit) for i in range(size)])
+
+
+def bits_of(size):
+    return [1 << i for i in range(size.bit_length() - 1)]
+
+
+def sum_all(value, sizes):
+    for bit in bits_of(sizes["dp"]):
+        value = value + swap(value, "dp", bit, sizes["dp"])
+    return value + swap(value, "fsdp", 1, 2)
+
+
+def gather_shard(shard):
+    other = swap(shard, "fsdp", 1, 2)
+    first = lax.axis_index("fsdp") == 0
+    return jnp.concatenate([jnp.where(first, shard, other), jnp.where(first, other, shard)], axis=0)
+
+
+def split_half(value, index):
+    half = value.shape[0] // 2
+    keep = lax.dynamic_slice_in_dim(value, index * half, half, axis=0)
+    send = lax.dynamic_slice_in_dim(value, (1 - index) * half, half, axis=0)
+    return keep, send
+
+
+def reduce_rows(value, sizes):
+    f32 = jnp.float32
+    dp = lax.axis_index("dp")
+    core, x = dp & 1, lax.axis_index("fsdp")
+    keep = lax.dynamic_index_in_dim(value, core, 1, keepdims=False)
+    send = lax.dynamic_index_in_dim(value, 1 - core, 1, keepdims=False)
+    got = swap(send, "dp", 1, sizes["dp"])
+    keep = (keep.astype(f32) + got.astype(f32)).astype(jnp.bfloat16)
+    keep, send = split_half(keep, x)
+    keep, send = keep[0], send[0]
+    got = swap(send, "fsdp", 1, 2)
+    keep = (keep.astype(f32) + got.astype(f32)).astype(jnp.bfloat16)
+    bits = bits_of(sizes["dp"])[1:]
+    for bit in bits:
+        index = ((dp & bit) > 0).astype(jnp.int32)
+        keep, send = split_half(keep, index)
+        got = swap(send, "dp", bit, sizes["dp"])
+        keep = (keep.astype(f32) + got.astype(f32)).astype(jnp.bfloat16)
+    for bit in bits[::-1] + [1]:
+        low = (dp & bit) == 0
+        got = swap(keep, "dp", bit, sizes["dp"])
+        keep = jnp.concatenate([jnp.where(low, keep, got), jnp.where(low, got, keep)], axis=0)
+    return keep.reshape(2, -1, 512)
 
 
 def product(left, right):
@@ -170,7 +222,7 @@
 
 
 def conv_forward(
-    values, gain, w_in, kernel, batch_gain_part, batch_bias_part, w_out, segment, valid_frames
+    values, gain, w_in, kernel, batch_gain_part, batch_bias_part, w_out, segment, valid_frames, sizes
 ):
     normed, normal_rows, inverse_deviation = normalize(values, gain)
     entry_value = normed.astype(jnp.bfloat16)
@@ -188,9 +240,8 @@
         jnp.sum(mixed_rows * mixed_rows * valid_frames[:, None], axis=0),
         jnp.sum(valid_frames),
     )
-    sum_first, sum_second, frame_count = lax.psum(
-        (local_sums[0], local_sums[1], local_sums[2]), ("dp", "fsdp")
-    )
+    packed = jnp.stack([local_sums[0], local_sums[1], jnp.full_like(local_sums[0], local_sums[2])])
+    sum_first, sum_second, frame_count = sum_all(packed, sizes)
     centered_rows = sum_first / frame_count
     batch_inverse_std = lax.rsqrt(sum_second / frame_count - centered_rows * centered_rows + EPS)
     normalized_input = (mixed_rows - centered_rows) * batch_inverse_std
@@ -213,7 +264,7 @@
 
 
 def conv_back(
-    grad_state, gain, w_in, kernel, batch_gain_part, w_out, segment, valid_frames, saved_tensors
+    grad_state, gain, w_in, kernel, batch_gain_part, w_out, segment, valid_frames, saved_tensors, sizes
 ):
     (
         entry_value,
@@ -233,8 +284,8 @@
     batch_gradient = product_nt(grad_branch, w_out) * swish_grad(batch_normed_rows)
     local_bias = jnp.sum(batch_gradient, axis=0)
     local_gain_sum = jnp.sum(batch_gradient * normalized_input, axis=0)
-    summed_bias_gradient, summed_gain_gradient = lax.psum(
-        (local_bias, local_gain_sum), ("dp", "fsdp")
+    summed_bias_gradient, summed_gain_gradient = sum_all(
+        jnp.stack([local_bias, local_gain_sum]), sizes
     )
     grad_mixed = batch_inverse_std * (
         batch_gradient * batch_gain_part
@@ -273,24 +324,7 @@
 
 
 def collect(shards):
-    return (
-        lax.all_gather(shards[0], "fsdp", axis=0, tiled=True),
-        lax.all_gather(shards[1], "fsdp", axis=0, tiled=True),
-        lax.all_gather(shards[2], "fsdp", axis=0, tiled=True),
-        lax.all_gather(shards[3], "fsdp", axis=0, tiled=True),
-        lax.all_gather(shards[4], "fsdp", axis=0, tiled=True),
-        lax.all_gather(shards[5], "fsdp", axis=0, tiled=True),
-        lax.all_gather(shards[6], "fsdp", axis=0, tiled=True),
-        lax.all_gather(shards[7], "fsdp", axis=0, tiled=True),
-        lax.all_gather(shards[8], "fsdp", axis=0, tiled=True),
-        lax.all_gather(shards[9], "fsdp", axis=0, tiled=True),
-        lax.all_gather(shards[10], "fsdp", axis=0, tiled=True),
-        lax.all_gather(shards[11], "fsdp", axis=0, tiled=True),
-        lax.all_gather(shards[12], "fsdp", axis=0, tiled=True),
-        lax.all_gather(shards[13], "fsdp", axis=0, tiled=True),
-        lax.all_gather(shards[14], "fsdp", axis=0, tiled=True),
-        lax.all_gather(shards[15], "fsdp", axis=0, tiled=True),
-    )
+    return tuple(gather_shard(shard) for shard in shards)
 
 
 def add_tuples(first_set, second_set):
@@ -298,6 +332,7 @@
 
 
 def body(
+    sizes,
     frames,
     item_lengths,
     frame_mask,
@@ -339,10 +374,10 @@
     )
     slots = frames.shape[1]
     parts = None
+    full = collect(shards)
     outputs = []
     input_grads = []
     for micro in range(MB):
-        full = collect(shards)
         (
             norm_one,
             up_one,
@@ -386,48 +421,13 @@
             out_conv,
             segment,
             valid_frames,
+            sizes,
         )
         after_conv = after_attend + branch
         branch, saved_two = feed_forward(after_conv, norm_two.astype(jnp.float32), up_two, down_two)
         after_two = after_conv + 0.5 * branch
         final_out, final_normal, final_inv = normalize(after_two, norm_last.astype(jnp.float32))
         outputs.append(final_out.astype(jnp.bfloat16))
-        back_full = (
-            lax.all_gather(shards[0], "fsdp", axis=0, tiled=True),
-            lax.all_gather(shards[1], "fsdp", axis=0, tiled=True),
-            lax.all_gather(shards[2], "fsdp", axis=0, tiled=True),
-            lax.all_gather(shards[3], "fsdp", axis=0, tiled=True),
-            lax.all_gather(shards[4], "fsdp", axis=0, tiled=True),
-            lax.all_gather(shards[5], "fsdp", axis=0, tiled=True),
-            lax.all_gather(shards[6], "fsdp", axis=0, tiled=True),
-            lax.all_gather(shards[7], "fsdp", axis=0, tiled=True),
-            lax.all_gather(shards[8], "fsdp", axis=0, tiled=True),
-            lax.all_gather(shards[9], "fsdp", axis=0, tiled=True),
-            lax.all_gather(shards[10], "fsdp", axis=0, tiled=True),
-            lax.all_gather(shards[11], "fsdp", axis=0, tiled=True),
-            lax.all_gather(shards[12], "fsdp", axis=0, tiled=True),
-            lax.all_gather(shards[13], "fsdp", axis=0, tiled=True),
-            lax.all_gather(shards[14], "fsdp", axis=0, tiled=True),
-            lax.all_gather(shards[15], "fsdp", axis=0, tiled=True),
-        )
-        (
-            norm_one,
-            up_one,
-            down_one,
-            norm_attend,
-            joint_attend,
-            out_attend,
-            norm_conv,
-            in_conv,
-            kernel_conv,
-            batch_gain_part,
-            batch_bias_part,
-            out_conv,
-            norm_two,
-            up_two,
-            down_two,
-            norm_last,
-        ) = back_full
         grad_state, grad_last = normalize_back(
             output_grad[micro].astype(jnp.float32),
             final_normal,
@@ -447,6 +447,7 @@
             segment,
             valid_frames,
             saved_conv,
+            sizes,
         )
         grad_state, grads_attend = attend_back(
             grad_state,
@@ -480,58 +481,28 @@
             grads_two[2],
             grad_last,
         )
-        piece = (
-            lax.psum_scatter(
-                grads[0].astype(jnp.bfloat16), "fsdp", scatter_dimension=0, tiled=True
-            ).astype(jnp.float32),
-            lax.psum_scatter(
-                grads[1].astype(jnp.bfloat16), "fsdp", scatter_dimension=0, tiled=True
-            ).astype(jnp.float32),
-            lax.psum_scatter(
-                grads[2].astype(jnp.bfloat16), "fsdp", scatter_dimension=0, tiled=True
-            ).astype(jnp.float32),
-            lax.psum_scatter(
-                grads[3].astype(jnp.bfloat16), "fsdp", scatter_dimension=0, tiled=True
-            ).astype(jnp.float32),
-            lax.psum_scatter(
-                grads[4].astype(jnp.bfloat16), "fsdp", scatter_dimension=0, tiled=True
-            ).astype(jnp.float32),
-            lax.psum_scatter(
-                grads[5].astype(jnp.bfloat16), "fsdp", scatter_dimension=0, tiled=True
-            ).astype(jnp.float32),
-            lax.psum_scatter(
-                grads[6].astype(jnp.bfloat16), "fsdp", scatter_dimension=0, tiled=True
-            ).astype(jnp.float32),
-            lax.psum_scatter(
-                grads[7].astype(jnp.bfloat16), "fsdp", scatter_dimension=0, tiled=True
-            ).astype(jnp.float32),
-            lax.psum_scatter(
-                grads[8].astype(jnp.bfloat16), "fsdp", scatter_dimension=0, tiled=True
-            ).astype(jnp.float32),
-            lax.psum_scatter(
-                grads[9].astype(jnp.bfloat16), "fsdp", scatter_dimension=0, tiled=True
-            ).astype(jnp.float32),
-            lax.psum_scatter(
-                grads[10].astype(jnp.bfloat16), "fsdp", scatter_dimension=0, tiled=True
-            ).astype(jnp.float32),
-            lax.psum_scatter(
-                grads[11].astype(jnp.bfloat16), "fsdp", scatter_dimension=0, tiled=True
-            ).astype(jnp.float32),
-            lax.psum_scatter(
-                grads[12].astype(jnp.bfloat16), "fsdp", scatter_dimension=0, tiled=True
-            ).astype(jnp.float32),
-            lax.psum_scatter(
-                grads[13].astype(jnp.bfloat16), "fsdp", scatter_dimension=0, tiled=True
-            ).astype(jnp.float32),
-            lax.psum_scatter(
-                grads[14].astype(jnp.bfloat16), "fsdp", scatter_dimension=0, tiled=True
-            ).astype(jnp.float32),
-            lax.psum_scatter(
-                grads[15].astype(jnp.bfloat16), "fsdp", scatter_dimension=0, tiled=True
-            ).astype(jnp.float32),
-        )
-        parts = piece if parts is None else add_tuples(parts, piece)
-    totals = lax.psum(parts, "dp")
+        parts = grads if parts is None else add_tuples(parts, grads)
+    big = [1, 2, 4, 5, 7, 11, 13, 14]
+    small = [i for i in range(16) if i not in big]
+    packed = jnp.concatenate(
+        [parts[i].astype(jnp.bfloat16).reshape(2, 2, -1, 512) for i in big], axis=2
+    )
+    reduced = reduce_rows(packed, sizes).astype(jnp.float32)
+    totals = [None] * 16
+    at = 0
+    for i in big:
+        rows, columns = parts[i].shape
+        count = rows * columns // 2048
+        totals[i] = reduced[:, at : at + count].reshape(rows // 2, columns)
+        at += count
+    flat = sum_all(jnp.concatenate([parts[i].reshape(-1, 512) for i in small], axis=0), sizes)
+    at = 0
+    for i in small:
+        count = parts[i].size // 512
+        whole = flat[at : at + count].reshape(parts[i].shape)
+        half = parts[i].shape[0] // 2
+        totals[i] = lax.dynamic_slice_in_dim(whole, lax.axis_index("fsdp") * half, half, axis=0)
+        at += count
     return (
         jnp.stack(outputs),
         jnp.stack(input_grads),
@@ -555,8 +526,9 @@
 
 
 def solution(mesh):
+    sizes = dict(mesh.shape)
     return jax.shard_map(
-        body,
+        functools.partial(body, sizes),
         mesh=mesh,
         in_specs=(
             P(None, ("dp", "fsdp"), None),

time: 1040 us -> 701 us (0.67)
  blocking collectives: 217 us -> 0 us
  waiting for transfers between devices: 440 us -> 273 us
  starting transfers between devices: 2.19 us -> 54.6 us
  matrix products: 168 us -> 127 us
  local copies, waits for them, and re-layouts: 57.5 us -> 90.5 us
  other arithmetic: 129 us -> 146 us
  between operations: 21.3 us -> 5.86 us
    ppermute x0 -> x50, waiting for transfers between devices: none -> 273 us  [swap(): return lax.ppermute(value, axis, [(i, i ^ bit) for i in range(size)])]
    reduce_scatter x18 -> x0, waiting for transfers between devices: 255 us -> none  [the longest x2 65.6 us: body(): lax.psum_scatter(grads[1].astype(jnp.bfloat16), 'fsdp', scatter_dimension...]
    psum x1 -> x0, waiting for transfers between devices: 170 us -> none  [body(): totals = lax.psum(parts, 'dp')]
    psum x3 -> x0, blocking collectives: 147 us -> none  [the longest x1 64 us: body(): totals = lax.psum(parts, 'dp')]
    all_gather x10 -> x0, blocking collectives: 62.9 us -> none  [the longest x1 14.4 us: collect(): lax.all_gather(shards[5], 'fsdp', axis=0, tiled=True)]
    ppermute x0 -> x50, starting transfers between devices: none -> 54.6 us  [swap(): return lax.ppermute(value, axis, [(i, i ^ bit) for i in range(size)])]
    reshape x0 -> x8, local copies, waits for them, and re-layouts: none -> 24.4 us  [the longest x4 15.3 us: body(): parts[i].astype(jnp.bfloat16).reshape(2, 2, -1, 512)]
    add x16 -> x8, other arithmetic: 23 us -> 4.53 us  [add_tuples(): left_item + right_item]
  transfers between devices with their start and end apart: 25 -> 50, of which waited for: 11 -> 23; matrix products, arithmetic and copies ran while one was open for 27% -> 21% of each run, Pallas kernels for 0% -> 0%
where the time goes in v1:
time: 701 us; the launch traced here: 697 us
  waiting for transfers between devices  273 us (39%)
  other arithmetic  146 us (21%)
  matrix products  127 us (18%)
  local copies, waits for them, and re-layouts  90.5 us (13%)
  starting transfers between devices  54.6 us (8%)
    ppermute x50, waiting for transfers between devices, swap(): return lax.ppermute(value, axis, [(i, i ^ bit) for i in range(size)])  273 us
    ppermute x50, starting transfers between devices, swap(): return lax.ppermute(value, axis, [(i, i ^ bit) for i in range(size)])  54.6 us
    dot_general x16, matrix products, product_nt(): lax.dot_general(left, right, (((1,), (1,)), ((), ())), preferred_element_...  38.9 us
    dot_general x16, matrix products, product_tn(): lax.dot_general(left, right, (((0,), (0,)), ((), ())), preferred_element_...  38.2 us
    unnamed x683, local copies, waits for them, and re-layouts  35.7 us
    reduce_sum x8, other arithmetic, conv_back(): jnp.sum(grad_mixed * shifted(gated_linear_unit, shift_by, 0.0) * same_fwd...  21.3 us
    dot_general x16, matrix products, product(): return jnp.dot(left, right, preferred_element_type=jnp.float32)  21 us
    convert_element_type x5, other arithmetic, reduce_rows(): keep = (keep.astype(f32) + got.astype(f32)).astype(jnp.bfloat16)  17.4 us
  transfers between devices with their start and end apart: 50, of which 23 were waited for; matrix products, arithmetic and copies ran while one was open for 21% of the time, Pallas kernels for 0%

profile of v1, /device:TPU:0, one launch (start us, length us, event | category | flops | bytes accessed | tf_op | source)
XLA Modules:
  0.0 696.7 jit_solution(15981771739000699761)
XLA Ops:
  0.7 3.0 collective-permute-start
  44.3 2.6 collective-permute-done.16
  49.7 8.5 %collective-permute-done.8 = bf16[256,1024]{1,0:T(8,128)(2,1)S(1)} collective-permute-done((bf16[256,1024]{1,0:T(8,128)(2,1)}, bf16[256,1024]{1,0:T(8,128)(2,1)S(1)}, u32[]{:S(2)}, u32[]{:S(2)}) %collective-permute-start.8) | collective-permute-done | bytes 524320 | tf_op jit(solution)/shard_map/ppermute | solution.py:18
  61.3 13.8 %collective-permute-done.4 = bf16[256,1536]{1,0:T(8,128)(2,1)S(1)} collective-permute-done((bf16[256,1536]{1,0:T(8,128)(2,1)}, bf16[256,1536]{1,0:T(8,128)(2,1)S(1)}, u32[]{:S(2)}, u32[]{:S(2)}) %collective-permute-start.4) | collective-permute-done | bytes 786464 | tf_op jit(solution)/shard_map/ppermute | solution.py:18
  76.3 21.2 %collective-permute-done.1 = bf16[256,2048]{1,0:T(8,128)(2,1)S(1)} collective-permute-done((bf16[256,2048]{1,0:T(8,128)(2,1)}, bf16[256,2048]{1,0:T(8,128)(2,1)S(1)}, u32[]{:S(2)}, u32[]{:S(2)}) %collective-permute-start.1) | collective-permute-done | bytes 1048608 | tf_op jit(solution)/shard_map/ppermute | solution.py:18
  99.1 20.9 %collective-permute-done.2 = bf16[1024,512]{1,0:T(8,128)(2,1)S(1)} collective-permute-done((bf16[1024,512]{1,0:T(8,128)(2,1)}, bf16[1024,512]{1,0:T(8,128)(2,1)S(1)}, u32[]{:S(2)}, u32[]{:S(2)}) %collective-permute-start.2) | collective-permute-done | bytes 1048608 | tf_op jit(solution)/shard_map/ppermute | solution.py:18
  141.2 7.0 %multiply_reduce_fusion.89 = (f32[512]{0:T(512)S(1)}, f32[512]{0:T(512)S(1)}, f32[512,512]{1,0:T(8,128)S(1)}) fusion(f32[512]{0:T(512)S(1)} %bitcast.393, f32[512]{0:T(512)S(1)} %copy-done.301, f32[512]{0:T(512)} %bitcast.42, f32[512]{0:T(512)S(1)} %copy-done.208, f32[512]{0:T(512)} %bitcast.41, f32[512]{0:T(512)S(1)} %copy-done.210, f32[512]{0:T(512)} %bitcast.40, ...), kind=kLoop, calls=%fused_computation.607 | loop fusion | flops 25951232 | bytes 2232320 | tf_op jit(solution)/shard_map/reduce_sum | solution.py:239
  160.1 7.3 %multiply_reduce_fusion.83 = (f32[512]{0:T(512)S(1)}, f32[512]{0:T(512)S(1)}, f32[512,512]{1,0:T(8,128)S(1)}) fusion(f32[512]{0:T(512)S(1)} %bitcast.389, f32[512]{0:T(512)S(1)} %copy-done.299, f32[512]{0:T(512)} %bitcast.42, f32[512]{0:T(512)S(1)} %copy-done.192, f32[512]{0:T(512)} %bitcast.41, f32[512]{0:T(512)S(1)} %copy-done.194, f32[512]{0:T(512)} %bitcast.40, ...), kind=kLoop, calls=%fused_computation.592 | loop fusion | flops 25951232 | bytes 2232320 | tf_op jit(solution)/shard_map/reduce_sum | solution.py:239
  178.6 3.0 collective-permute-start.12
  194.1 2.4 multiply_convert_fusion.5
  207.5 2.5 multiply_add_fusion.5
  209.9 2.4 multiply_convert_fusion.3
  212.3 3.4 add_convert_fusion
  219.3 2.5 fusion.514
  221.9 2.9 fusion.513
  232.2 2.7 add_convert_fusion.1
  245.9 4.4 reshape.995
  252.7 4.7 multiply_reduce_fusion.36
  257.6 7.5 %multiply_convert_fusion.16 = (bf16[512,512]{1,0:T(8,128)(2,1)S(1)}, f32[512,512]{1,0:T(8,128)S(1)}) fusion(f32[512,1024]{1,0:T(8,128)S(1)} %copy-done.13, f32[512]{0:T(512)S(1)} %bitcast.395, f32[512]{0:T(512)S(1)} %copy-done.312, f32[512]{0:T(512)} %bitcast.42, f32[512]{0:T(512)S(1)} %copy-done.267, f32[512]{0:T(512)} %bitcast.41, f32[512]{0:T(512)S(1)} %copy-done.279, ...), kind=kLoop, calls=%fused_computation.579 | loop fusion | flops 26214400 | bytes 3801088 | tf_op jit(solution)/shard_map/convert.29
  269.7 3.9 multiply_reduce_fusion.4
  273.8 7.8 %multiply_convert_fusion.12 = (bf16[512,512]{1,0:T(8,128)(2,1)S(1)}, f32[512,512]{1,0:T(8,128)S(1)}) fusion(f32[512,1024]{1,0:T(8,128)S(1)} %copy-done.11, f32[512]{0:T(512)S(1)} %bitcast.391, f32[512]{0:T(512)S(1)} %copy-done.311, f32[512]{0:T(512)} %bitcast.42, f32[512]{0:T(512)S(1)} %copy-done.254, f32[512]{0:T(512)} %bitcast.41, f32[512]{0:T(512)S(1)} %copy-done.265, ...), kind=kLoop, calls=%fused_computation.568 | loop fusion | flops 26214400 | bytes 3801088 | tf_op jit(solution)/shard_map/convert.16
  282.1 2.6 multiply_reduce_fusion.68
  289.4 2.9 fusion.55
  292.3 5.9 multiply_reduce_fusion
  298.3 4.7 multiply_convert_fusion
  307.1 2.9 fusion.58
  310.0 3.6 multiply_reduce_fusion.1
  313.7 2.9 multiply_convert_fusion.1
  322.7 2.7 fusion.507
  327.4 2.9 multiply_reduce_fusion.70
  330.6 5.1 multiply_convert_fusion.4
  335.7 3.5 fusion.319
  339.3 2.4 add_convert_fusion.5
  344.0 3.1 fusion.41
  347.2 3.6 fusion.18
  350.8 4.1 reshape.991
  357.7 4.1 multiply_convert_fusion.2
  361.8 3.1 add_convert_fusion.2
  366.3 2.7 add_convert_fusion.3
  369.0 4.5 reshape.989
  380.1 3.2 dynamic-slice_bitcast_fusion
  383.3 3.0 copy-done.25
  386.3 10.1 %collective-permute-done.41 = bf16[2,2944,512]{2,1,0:T(8,128)(2,1)} collective-permute-done((bf16[2,2944,512]{2,1,0:T(8,128)(2,1)}, bf16[2,2944,512]{2,1,0:T(8,128)(2,1)}, u32[]{:S(2)}, u32[]{:S(2)}) %collective-permute-start.41) | collective-permute-done | bytes 6029344 | tf_op jit(solution)/shard_map/ppermute | solution.py:18
  396.4 8.7 %fusion = bf16[2,2944,512]{2,1,0:T(8,128)(2,1)} fusion(bf16[2,2944,512]{2,1,0:T(8,128)(2,1)} %collective-permute-done.41, bf16[2,2,2944,512]{3,2,1,0:T(8,128)(2,1)} %copy-done.25, s32[]{:T(128)S(6)} %select_n.305), kind=kLoop, calls=%fused_computation.1 | loop fusion | flops 12058624 | bytes 18087940 | tf_op jit(solution)/shard_map/convert_element_type | solution.py:51
  405.1 3.7 dynamic-slice_bitcast_fusion.1
  409.4 67.1 %collective-permute-done.42 = bf16[2944,512]{1,0:T(8,128)(2,1)} collective-permute-done((bf16[2944,512]{1,0:T(8,128)(2,1)}, bf16[2944,512]{1,0:T(8,128)(2,1)}, u32[]{:S(2)}, u32[]{:S(2)}) %collective-permute-start.42) | collective-permute-done | bytes 3014688 | tf_op jit(solution)/shard_map/ppermute | solution.py:18
  476.5 3.6 fusion.3
  483.6 33.8 %collective-permute-done.43 = bf16[1472,512]{1,0:T(8,128)(2,1)} collective-permute-done((bf16[1472,512]{1,0:T(8,128)(2,1)}, bf16[1472,512]{1,0:T(8,128)(2,1)}, u32[]{:S(2)}, u32[]{:S(2)}) %collective-permute-start.43) | collective-permute-done | bytes 1507360 | tf_op jit(solution)/shard_map/ppermute | solution.py:18
  522.2 17.0 %collective-permute-done.44 = bf16[736,512]{1,0:T(8,128)(2,1)} collective-permute-done((bf16[736,512]{1,0:T(8,128)(2,1)}, bf16[736,512]{1,0:T(8,128)(2,1)}, u32[]{:S(2)}, u32[]{:S(2)}) %collective-permute-start.44) | collective-permute-done | bytes 753696 | tf_op jit(solution)/shard_map/ppermute | solution.py:18
  547.3 11.6 %collective-permute-done.45 = bf16[368,512]{1,0:T(8,128)(2,1)} collective-permute-done((bf16[368,512]{1,0:T(8,128)(2,1)S(1)}, bf16[368,512]{1,0:T(8,128)(2,1)}, u32[]{:S(2)}, u32[]{:S(2)}) %collective-permute-start.45) | collective-permute-done | bytes 376864 | tf_op jit(solution)/shard_map/ppermute | solution.py:18
  560.3 3.1 multiply_reduce_fusion.54
  563.5 13.9 %collective-permute-done.46 = bf16[368,512]{1,0:T(8,128)(2,1)S(1)} collective-permute-done((bf16[368,512]{1,0:T(8,128)(2,1)S(1)}, bf16[368,512]{1,0:T(8,128)(2,1)S(1)}, u32[]{:S(2)}, u32[]{:S(2)}) %collective-permute-start.46) | collective-permute-done | bytes 376864 | tf_op jit(solution)/shard_map/ppermute | solution.py:18
  580.9 2.4 multiply_reduce_fusion.45
  583.2 3.0 stack.342
  588.2 10.0 %collective-permute-done.47 = bf16[736,512]{1,0:T(8,128)(2,1)} collective-permute-done((bf16[736,512]{1,0:T(8,128)(2,1)}, bf16[736,512]{1,0:T(8,128)(2,1)}, u32[]{:S(2)}, u32[]{:S(2)}) %collective-permute-start.47) | collective-permute-done | bytes 753696 | tf_op jit(solution)/shard_map/ppermute | solution.py:18
  608.4 3.8 fusion.267
  612.2 24.6 %collective-permute-done.48 = bf16[1472,512]{1,0:T(8,128)(2,1)} collective-permute-done((bf16[1472,512]{1,0:T(8,128)(2,1)}, bf16[1472,512]{1,0:T(8,128)(2,1)}, u32[]{:S(2)}, u32[]{:S(2)}) %collective-permute-start.48) | collective-permute-done | bytes 1507360 | tf_op jit(solution)/shard_map/ppermute | solution.py:18
  652.2 3.1 collective-permute-done.37
  655.9 3.9 collective-permute-done.38
  662.4 3.7 collective-permute-done.39
  675.3 4.0 broadcast_select_fusion.1
  684.1 3.2 fusion.519
  688.6 2.8 reshape.999
  691.4 3.2 reshape.1003
  (1007 shorter events, 243.0 us)
Async XLA Ops:
  0.7 27.1 %collective-permute-start = (bf16[256]{0:T(256)(128)(2,1)}, bf16[256]{0:T(256)(128)(2,1)}, u32[]{:S(2)}, u32[]{:S(2)}) collective-permute-start(bf16[256]{0:T(256)(128)(2,1)} %param.23), channel_id=1, source_target_pairs={{0,1},{1,0},{2,3},{3,2},{4,5},{5,4},{6,7},{7,6},{8,9},{9,8},{10,11... | collective-permute-start | bytes 1544 | tf_op jit(solution)/shard_map/ppermute | solution.py:18
  3.7 24.8 %collective-permute-start.3 = (bf16[256]{0:T(256)(128)(2,1)}, bf16[256]{0:T(256)(128)(2,1)}, u32[]{:S(2)}, u32[]{:S(2)}) collective-permute-start(bf16[256]{0:T(256)(128)(2,1)} %param.26), channel_id=1, source_target_pairs={{0,1},{1,0},{2,3},{3,2},{4,5},{5,4},{6,7},{7,6},{8,9},{9,8},{10,11... | collective-permute-start | bytes 1544 | tf_op jit(solution)/shard_map/ppermute | solution.py:18
  3.8 26.8 %collective-permute-start.7 = (bf16[256]{0:T(256)(128)(2,1)}, bf16[256]{0:T(256)(128)(2,1)}, u32[]{:S(2)}, u32[]{:S(2)}) collective-permute-start(bf16[256]{0:T(256)(128)(2,1)} %param.29), channel_id=1, source_target_pairs={{0,1},{1,0},{2,3},{3,2},{4,5},{5,4},{6,7},{7,6},{8,9},{9,8},{10,11... | collective-permute-start | bytes 1544 | tf_op jit(solution)/shard_map/ppermute | solution.py:18
  5.7 26.1 %collective-permute-start.14 = (bf16[256]{0:T(256)(128)(2,1)}, bf16[256]{0:T(256)(128)(2,1)}, u32[]{:S(2)}, u32[]{:S(2)}) collective-permute-start(bf16[256]{0:T(256)(128)(2,1)} %param.32), channel_id=1, source_target_pairs={{0,1},{1,0},{2,3},{3,2},{4,5},{5,4},{6,7},{7,6},{8,9},{9,8},{10,11... | collective-permute-start | bytes 1544 | tf_op jit(solution)/shard_map/ppermute | solution.py:18
  5.8 28.1 %collective-permute-start.15 = (bf16[256]{0:T(256)(128)(2,1)}, bf16[256]{0:T(256)(128)(2,1)}, u32[]{:S(2)}, u32[]{:S(2)}) collective-permute-start(bf16[256]{0:T(256)(128)(2,1)} %param.33), channel_id=1, source_target_pairs={{0,1},{1,0},{2,3},{3,2},{4,5},{5,4},{6,7},{7,6},{8,9},{9,8},{10,11... | collective-permute-start | bytes 1544 | tf_op jit(solution)/shard_map/ppermute | solution.py:18
  19.4 103.8 %copy-start.17 = (bf16[1,512,512]{1,2,0:T(8,128)(2,1)}, bf16[1,512,512]{1,2,0:T(8,128)(2,1)S(1)}, u32[]{:S(2)}) copy-start(bf16[1,512,512]{1,2,0:T(8,128)(2,1)S(1)} %copy.98) | copy-start | bytes 1572868
  19.5 102.2 %copy-start.142 = (f32[512]{0:T(512)}, f32[512]{0:T(512)S(1)}, u32[]{:S(2)}) copy-start(f32[512]{0:T(512)S(1)} %broadcast_multiply_fusion.31) | copy-start | bytes 6148
  19.7 102.0 %copy-start.146 = (f32[512]{0:T(512)}, f32[512]{0:T(512)S(1)}, u32[]{:S(2)}) copy-start(f32[512]{0:T(512)S(1)} %add_rsqrt_fusion.11) | copy-start | bytes 6148
  20.0 100.2 %copy-start.14 = (bf16[1,512,512]{1,2,0:T(8,128)(2,1)}, bf16[1,512,512]{1,2,0:T(8,128)(2,1)S(1)}, u32[]{:S(2)}) copy-start(bf16[1,512,512]{1,2,0:T(8,128)(2,1)S(1)} %copy.99) | copy-start | bytes 1572868
  21.3 111.5 %copy-start.44 = (pred[512,512]{0,1:T(8,128)(4,1)}, pred[512,512]{0,1:T(8,128)(4,1)S(1)}, u32[]{:S(2)}) copy-start(pred[512,512]{0,1:T(8,128)(4,1)S(1)} %get-tuple-element.443) | copy-start | bytes 786436
  23.3 105.1 %copy-start.124 = (f32[512,32]{0,1:T(8,128)}, f32[512,32]{0,1:T(8,128)S(1)}, u32[]{:S(2)}) copy-start(f32[512,32]{0,1:T(8,128)S(1)} %get-tuple-element.307) | copy-start | bytes 196612
  23.3 125.1 %copy-start.122 = (f32[512,32]{0,1:T(8,128)}, f32[512,32]{0,1:T(8,128)S(1)}, u32[]{:S(2)}) copy-start(f32[512,32]{0,1:T(8,128)S(1)} %get-tuple-element.402) | copy-start | bytes 196612
  27.8 7.5 %collective-permute-start.17 = (bf16[256]{0:T(256)(128)(2,1)}, bf16[256]{0:T(256)(128)(2,1)S(1)}, u32[]{:S(2)}, u32[]{:S(2)}) collective-permute-start(bf16[256]{0:T(256)(128)(2,1)} %param.35), channel_id=1, source_target_pairs={{0,1},{1,0},{2,3},{3,2},{4,5},{5,4},{6,7},{7,6},{8,9},{9,8},{10,11... | collective-permute-start | bytes 1544 | tf_op jit(solution)/shard_map/ppermute | solution.py:18
  28.5 93.3 %copy-start.129 = (f32[512]{0:T(512)}, f32[512]{0:T(512)S(1)}, u32[]{:S(2)}) copy-start(f32[512]{0:T(512)S(1)} %maximum_convert_fusion.2) | copy-start | bytes 6148
  28.5 8.7 %collective-permute-start.20 = (bf16[256]{0:T(256)(128)(2,1)}, bf16[256]{0:T(256)(128)(2,1)S(1)}, u32[]{:S(2)}, u32[]{:S(2)}) collective-permute-start(bf16[256]{0:T(256)(128)(2,1)} %param.38), channel_id=1, source_target_pairs={{0,1},{1,0},{2,3},{3,2},{4,5},{5,4},{6,7},{7,6},{8,9},{9,8},{10,11... | collective-permute-start | bytes 1544 | tf_op jit(solution)/shard_map/ppermute | solution.py:18
  30.5 8.6 %collective-permute-start.6 = (bf16[16,512]{1,0:T(8,128)(2,1)}, bf16[16,512]{1,0:T(8,128)(2,1)S(1)}, u32[]{:S(2)}, u32[]{:S(2)}) collective-permute-start(bf16[16,512]{1,0:T(8,128)(2,1)} %param.31), channel_id=1, source_target_pairs={{0,1},{1,0},{2,3},{3,2},{4,5},{5,4},{6,7},{7,6},{8,9},{9,8},{10,11... | collective-permute-start | bytes 49160 | tf_op jit(solution)/shard_map/ppermute | solution.py:18
  31.9 95.1 %copy-start.131 = (f32[512]{0:T(512)}, f32[512]{0:T(512)S(1)}, u32[]{:S(2)}) copy-start(f32[512]{0:T(512)S(1)} %maximum_convert_fusion.3) | copy-start | bytes 6148
  31.9 11.3 %collective-permute-start.5 = (bf16[256,512]{1,0:T(8,128)(2,1)}, bf16[256,512]{1,0:T(8,128)(2,1)S(1)}, u32[]{:S(2)}, u32[]{:S(2)}) collective-permute-start(bf16[256,512]{1,0:T(8,128)(2,1)} %param.28), channel_id=1, source_target_pairs={{0,1},{1,0},{2,3},{3,2},{4,5},{5,4},{6,7},{7,6},{8,9},{9,8},{10,11... | collective-permute-start | bytes 786440 | tf_op jit(solution)/shard_map/ppermute | solution.py:18
  33.9 13.1 %collective-permute-start.16 = (bf16[256,512]{1,0:T(8,128)(2,1)}, bf16[256,512]{1,0:T(8,128)(2,1)S(1)}, u32[]{:S(2)}, u32[]{:S(2)}) collective-permute-start(bf16[256,512]{1,0:T(8,128)(2,1)} %param.34), channel_id=1, source_target_pairs={{0,1},{1,0},{2,3},{3,2},{4,5},{5,4},{6,7},{7,6},{8,9},{9,8},{10,11... | collective-permute-start | bytes 786440 | tf_op jit(solution)/shard_map/ppermute | solution.py:18
  35.3 22.9 %collective-permute-start.8 = (bf16[256,1024]{1,0:T(8,128)(2,1)}, bf16[256,1024]{1,0:T(8,128)(2,1)S(1)}, u32[]{:S(2)}, u32[]{:S(2)}) collective-permute-start(bf16[256,1024]{1,0:T(8,128)(2,1)} %param.30), channel_id=1, source_target_pairs={{0,1},{1,0},{2,3},{3,2},{4,5},{5,4},{6,7},{7,6},{8,9},{9,8},{10,11... | collective-permute-start | bytes 1572872 | tf_op jit(solution)/shard_map/ppermute | solution.py:18
  37.2 37.8 %collective-permute-start.4 = (bf16[256,1536]{1,0:T(8,128)(2,1)}, bf16[256,1536]{1,0:T(8,128)(2,1)S(1)}, u32[]{:S(2)}, u32[]{:S(2)}) collective-permute-start(bf16[256,1536]{1,0:T(8,128)(2,1)} %param.27), channel_id=1, source_target_pairs={{0,1},{1,0},{2,3},{3,2},{4,5},{5,4},{6,7},{7,6},{8,9},{9,8},{10,11... | collective-permute-start | bytes 2359304 | tf_op jit(solution)/shard_map/ppermute | solution.py:18
  39.1 58.4 %collective-permute-start.1 = (bf16[256,2048]{1,0:T(8,128)(2,1)}, bf16[256,2048]{1,0:T(8,128)(2,1)S(1)}, u32[]{:S(2)}, u32[]{:S(2)}) collective-permute-start(bf16[256,2048]{1,0:T(8,128)(2,1)} %param.24), channel_id=1, source_target_pairs={{0,1},{1,0},{2,3},{3,2},{4,5},{5,4},{6,7},{7,6},{8,9},{9,8},{10,11... | collective-permute-start | bytes 3145736 | tf_op jit(solution)/shard_map/ppermute | solution.py:18
  43.1 76.8 %collective-permute-start.2 = (bf16[1024,512]{1,0:T(8,128)(2,1)}, bf16[1024,512]{1,0:T(8,128)(2,1)S(1)}, u32[]{:S(2)}, u32[]{:S(2)}) collective-permute-start(bf16[1024,512]{1,0:T(8,128)(2,1)} %param.25), channel_id=1, source_target_pairs={{0,1},{1,0},{2,3},{3,2},{4,5},{5,4},{6,7},{7,6},{8,9},{9,8},{10,11... | collective-permute-start | bytes 3145736 | tf_op jit(solution)/shard_map/ppermute | solution.py:18
  44.3 111.4 %copy-start.46 = (bf16[256,512]{1,0:T(8,128)(2,1)}, bf16[256,512]{1,0:T(8,128)(2,1)S(1)}, u32[]{:S(2)}) copy-start(bf16[256,512]{1,0:T(8,128)(2,1)S(1)} %get-tuple-element.246) | copy-start | bytes 786436
  44.3 111.4 %copy-start.48 = (bf16[256,512]{1,0:T(8,128)(2,1)}, bf16[256,512]{1,0:T(8,128)(2,1)S(1)}, u32[]{:S(2)}) copy-start(bf16[256,512]{1,0:T(8,128)(2,1)S(1)} %get-tuple-element.247) | copy-start | bytes 786436
  46.9 121.1 %collective-permute-start.18 = (bf16[256,2048]{1,0:T(8,128)(2,1)}, bf16[256,2048]{1,0:T(8,128)(2,1)}, u32[]{:S(2)}, u32[]{:S(2)}) collective-permute-start(bf16[256,2048]{1,0:T(8,128)(2,1)} %param.36), channel_id=1, source_target_pairs={{0,1},{1,0},{2,3},{3,2},{4,5},{5,4},{6,7},{7,6},{8,9},{9,8},{10,11... | collective-permute-start | bytes 3145736 | tf_op jit(solution)/shard_map/ppermute | solution.py:18
  58.2 111.3 %collective-permute-start.19 = (bf16[1024,512]{1,0:T(8,128)(2,1)}, bf16[1024,512]{1,0:T(8,128)(2,1)}, u32[]{:S(2)}, u32[]{:S(2)}) collective-permute-start(bf16[1024,512]{1,0:T(8,128)(2,1)} %param.37), channel_id=1, source_target_pairs={{0,1},{1,0},{2,3},{3,2},{4,5},{5,4},{6,7},{7,6},{8,9},{9,8},{10,11... | collective-permute-start | bytes 3145736 | tf_op jit(solution)/shard_map/ppermute | solution.py:18
  61.2 95.2 %copy-start.53 = (bf16[256,1024]{1,0:T(8,128)(2,1)}, bf16[256,1024]{1,0:T(8,128)(2,1)S(1)}, u32[]{:S(2)}) copy-start(bf16[256,1024]{1,0:T(8,128)(2,1)S(1)} %get-tuple-element.240) | copy-start | bytes 1572868
  61.2 95.2 %copy-start.55 = (bf16[256,1024]{1,0:T(8,128)(2,1)}, bf16[256,1024]{1,0:T(8,128)(2,1)S(1)}, u32[]{:S(2)}) copy-start(bf16[256,1024]{1,0:T(8,128)(2,1)S(1)} %get-tuple-element.241) | copy-start | bytes 1572868
  148.3 89.8 %copy-start.78 = (f32[512,512]{1,0:T(8,128)}, f32[512,512]{1,0:T(8,128)S(1)}, u32[]{:S(2)}) copy-start(f32[512,512]{1,0:T(8,128)S(1)} %get-tuple-element.186) | copy-start | bytes 3145732
  148.3 22.7 %collective-permute-start.9 = (f32[3,512]{1,0:T(4,128)S(1)}, f32[3,512]{1,0:T(4,128)S(1)}, u32[]{:S(2)}, u32[]{:S(2)}) collective-permute-start(f32[3,512]{1,0:T(4,128)S(1)} %maximum_maximum_fusion), channel_id=1, source_target_pairs={{0,2},{2,0},{4,6},{6,4},{8,10},{10,8},{12,14},{14,12},{16,18},{18,... | collective-permute-start | bytes 18440 | tf_op jit(solution)/shard_map/ppermute | solution.py:18
  167.6 5.5 collective-permute-start.21
  171.1 3.7 collective-permute-start.10
  173.2 3.7 collective-permute-start.22
  174.8 3.7 collective-permute-start.11
  176.9 4.6 collective-permute-start.23
  178.6 4.6 collective-permute-start.12
  181.6 4.6 collective-permute-start.24
  183.2 4.5 collective-permute-start.13
  186.2 15.7 %collective-permute-start.25 = (f32[3,512]{1,0:T(4,128)S(1)}, f32[3,512]{1,0:T(4,128)S(1)}, u32[]{:S(2)}, u32[]{:S(2)}) collective-permute-start(f32[3,512]{1,0:T(4,128)S(1)} %add.980), channel_id=1, source_target_pairs={{0,1},{1,0},{2,3},{3,2},{4,5},{5,4},{6,7},{7,6},{8,9},{9,8},{10,11... | collective-permute-start | bytes 18440 | tf_op jit(solution)/shard_map/ppermute | solution.py:18
  221.8 3.5 collective-permute-start.31
  224.7 2.2 collective-permute-start.26
  225.3 3.7 collective-permute-start.32
  226.9 3.7 collective-permute-start.27
  229.0 6.0 collective-permute-start.33
  230.7 6.4 collective-permute-start.28
  235.0 4.6 collective-permute-start.34
  237.1 4.6 collective-permute-start.29
  240.1 10.3 %collective-permute-start.35 = (f32[2,512]{1,0:T(2,128)}, f32[2,512]{1,0:T(2,128)}, u32[]{:S(2)}, u32[]{:S(2)}) collective-permute-start(f32[2,512]{1,0:T(2,128)} %add.1045), channel_id=1, source_target_pairs={{0,1},{1,0},{2,3},{3,2},{4,5},{5,4},{6,7},{7,6},{8,9},{9,8},{10,11... | collective-permute-start | bytes 12296 | tf_op jit(solution)/shard_map/ppermute | solution.py:18
  242.3 9.0 %collective-permute-start.30 = (f32[2,512]{1,0:T(2,128)}, f32[2,512]{1,0:T(2,128)}, u32[]{:S(2)}, u32[]{:S(2)}) collective-permute-start(f32[2,512]{1,0:T(2,128)} %add.996), channel_id=1, source_target_pairs={{0,1},{1,0},{2,3},{3,2},{4,5},{5,4},{6,7},{7,6},{8,9},{9,8},{10,11... | collective-permute-start | bytes 12296 | tf_op jit(solution)/shard_map/ppermute | solution.py:18
  386.3 10.1 %collective-permute-start.41 = (bf16[2,2944,512]{2,1,0:T(8,128)(2,1)}, bf16[2,2944,512]{2,1,0:T(8,128)(2,1)}, u32[]{:S(2)}, u32[]{:S(2)}) collective-permute-start(bf16[2,2944,512]{2,1,0:T(8,128)(2,1)} %dynamic-slice_bitcast_fusion), channel_id=1, source_target_pairs={{0,2},{2,0},{4,6},{6,4},{8,10},{10,8},{12,14},{14,12},{16,18},{18,... | collective-permute-start | bytes 18087944 | tf_op jit(solution)/shard_map/ppermute | solution.py:18
  408.8 67.6 %collective-permute-start.42 = (bf16[2944,512]{1,0:T(8,128)(2,1)}, bf16[2944,512]{1,0:T(8,128)(2,1)}, u32[]{:S(2)}, u32[]{:S(2)}) collective-permute-start(bf16[2944,512]{1,0:T(8,128)(2,1)} %dynamic-slice_bitcast_fusion.1), channel_id=1, source_target_pairs={{0,1},{1,0},{2,3},{3,2},{4,5},{5,4},{6,7},{7,6},{8,9},{9,8},{10,11... | collective-permute-start | bytes 9043976 | tf_op jit(solution)/shard_map/ppermute | solution.py:18
  482.9 34.5 %collective-permute-start.43 = (bf16[1472,512]{1,0:T(8,128)(2,1)}, bf16[1472,512]{1,0:T(8,128)(2,1)}, u32[]{:S(2)}, u32[]{:S(2)}) collective-permute-start(bf16[1472,512]{1,0:T(8,128)(2,1)} %constant_dynamic-slice_fusion.8), channel_id=1, source_target_pairs={{0,4},{2,6},{4,0},{6,2},{8,12},{10,14},{12,8},{14,10},{16,20},{18,... | collective-permute-start | bytes 4521992 | tf_op jit(solution)/shard_map/ppermute | solution.py:18
  521.7 17.5 %collective-permute-start.44 = (bf16[736,512]{1,0:T(8,128)(2,1)}, bf16[736,512]{1,0:T(8,128)(2,1)}, u32[]{:S(2)}, u32[]{:S(2)}) collective-permute-start(bf16[736,512]{1,0:T(8,128)(2,1)} %constant_dynamic-slice_fusion.7), channel_id=1, source_target_pairs={{0,8},{2,10},{4,12},{6,14},{8,0},{10,2},{12,4},{14,6},{16,24},{18,... | collective-permute-start | bytes 2261000 | tf_op jit(solution)/shard_map/ppermute | solution.py:18
  541.6 17.3 %collective-permute-start.45 = (bf16[368,512]{1,0:T(8,128)(2,1)S(1)}, bf16[368,512]{1,0:T(8,128)(2,1)}, u32[]{:S(2)}, u32[]{:S(2)}) collective-permute-start(bf16[368,512]{1,0:T(8,128)(2,1)S(1)} %constant_dynamic-slice_fusion.6), channel_id=1, source_target_pairs={{0,16},{2,18},{4,20},{6,22},{8,24},{10,26},{12,28},{14,30},{16,0},... | collective-permute-start | bytes 1130504 | tf_op jit(solution)/shard_map/ppermute | solution.py:18
  560.2 17.1 %collective-permute-start.46 = (bf16[368,512]{1,0:T(8,128)(2,1)S(1)}, bf16[368,512]{1,0:T(8,128)(2,1)S(1)}, u32[]{:S(2)}, u32[]{:S(2)}) collective-permute-start(bf16[368,512]{1,0:T(8,128)(2,1)S(1)} %add_convert_fusion.7), channel_id=1, source_target_pairs={{0,16},{2,18},{4,20},{6,22},{8,24},{10,26},{12,28},{14,30},{16,0},... | collective-permute-start | bytes 1130504 | tf_op jit(solution)/shard_map/ppermute | solution.py:18
  579.1 19.1 %collective-permute-start.47 = (bf16[736,512]{1,0:T(8,128)(2,1)}, bf16[736,512]{1,0:T(8,128)(2,1)}, u32[]{:S(2)}, u32[]{:S(2)}) collective-permute-start(bf16[736,512]{1,0:T(8,128)(2,1)} %pad_maximum_fusion.15), channel_id=1, source_target_pairs={{0,8},{2,10},{4,12},{6,14},{8,0},{10,2},{12,4},{14,6},{16,24},{18,... | collective-permute-start | bytes 2261000 | tf_op jit(solution)/shard_map/ppermute | solution.py:18
  601.9 34.9 %collective-permute-start.48 = (bf16[1472,512]{1,0:T(8,128)(2,1)}, bf16[1472,512]{1,0:T(8,128)(2,1)}, u32[]{:S(2)}, u32[]{:S(2)}) collective-permute-start(bf16[1472,512]{1,0:T(8,128)(2,1)} %pad_maximum_fusion.9), channel_id=1, source_target_pairs={{0,4},{2,6},{4,0},{6,2},{8,12},{10,14},{12,8},{14,10},{16,20},{18,... | collective-permute-start | bytes 4521992 | tf_op jit(solution)/shard_map/ppermute | solution.py:18
  640.7 34.6 %collective-permute-start.49 = (bf16[2944,512]{1,0:T(8,128)(2,1)}, bf16[2944,512]{1,0:T(8,128)(2,1)}, u32[]{:S(2)}, u32[]{:S(2)}) collective-permute-start(bf16[2944,512]{1,0:T(8,128)(2,1)} %pad_maximum_fusion.1), channel_id=1, source_target_pairs={{0,2},{2,0},{4,6},{6,4},{8,10},{10,8},{12,14},{14,12},{16,18},{18,... | collective-permute-start | bytes 9043976 | tf_op jit(solution)/shard_map/ppermute | solution.py:18
  645.8 4.5 collective-permute-start.36
  650.4 4.9 collective-permute-start.37
  655.3 4.5 collective-permute-start.38
  659.8 6.3 collective-permute-start.39
  666.1 4.5 collective-permute-start.40
  (321 other events, 2611.5 us)

commit v2 on v1

v2 whole, which is shorter than its diff:
```python
import functools
import math

import jax
import jax.numpy as jnp
from jax import lax
from jax.experimental import pallas as pl
from jax.experimental.pallas import tpu as pltpu
from jax.sharding import PartitionSpec as P

HEADS = 8
KER = 32
HDIM = 64
MB = 2
D = 512
FF = 2048
EPS = 1e-05
PAD = 16
F32 = jnp.float32
BF16 = jnp.bfloat16
ANY = pl.BlockSpec(memory_space=pl.ANY)
SMEM = pl.BlockSpec(memory_space=pltpu.SMEM)


def swap(value, axis, bit, size):
    return lax.ppermute(value, axis, [(i, i ^ bit) for i in range(size)])


def bits_of(size):
    return [1 << i for i in range(size.bit_length() - 1)]


def sum_all(value, sizes):
    for bit in bits_of(sizes["dp"]):
        value = value + swap(value, "dp", bit, sizes["dp"])
    return value + swap(value, "fsdp", 1, 2)


def add_split(keep, got, index):
    half = keep.shape[0] // 2
    parts = []
    for at in (index, 1 - index):
        left = lax.dynamic_slice_in_dim(keep, at * half, half, axis=0)
        right = lax.dynamic_slice_in_dim(got, at * half, half, axis=0)
        parts.append((left.astype(F32) + right.astype(F32)).astype(BF16))
    return parts


def reduce_rows(send, keep, sizes):
    dp = lax.axis_index("dp")
    got = swap(send, "dp", 1, sizes["dp"])
    keep, send = add_split(keep, got, lax.axis_index("fsdp"))
    keep, send = keep[0], send[0]
    got = swap(send, "fsdp", 1, 2)
    bits = bits_of(sizes["dp"])[1:]
    for bit in bits:
        keep, send = add_split(keep, got, ((dp & bit) > 0).astype(jnp.int32))
        got = swap(send, "dp", bit, sizes["dp"])
    keep = (keep.astype(F32) + got.astype(F32)).astype(BF16)
    for bit in bits[::-1] + [1]:
        low = (dp & bit) == 0
        got = swap(keep, "dp", bit, sizes["dp"])
        keep = jnp.concatenate([jnp.where(low, keep, got), jnp.where(low, got, keep)], axis=0)
    return keep.reshape(2, -1, D)


def dot(left, right):
    return lax.dot_general(left, right, (((1,), (0,)), ((), ())), preferred_element_type=F32)


def dot_nt(left, right):
    return lax.dot_general(left, right, (((1,), (1,)), ((), ())), preferred_element_type=F32)


def dot_tn(left, right):
    return lax.dot_general(left, right, (((0,), (0,)), ((), ())), preferred_element_type=F32)


def sigmoid(values):
    return 0.5 * jnp.tanh(0.5 * values) + 0.5


def norm(values):
    centered = values - jnp.mean(values, axis=-1, keepdims=True)
    inverse = lax.rsqrt(jnp.mean(centered * centered, axis=-1, keepdims=True) + EPS)
    return centered * inverse, inverse


def norm_back(grad, rows, inverse, gain):
    scaled = grad * gain
    return inverse * (
        scaled
        - jnp.mean(scaled, axis=-1, keepdims=True)
        - rows * jnp.mean(scaled * rows, axis=-1, keepdims=True)
    )


def column_sum(values):
    return jnp.sum(values, axis=0, keepdims=True)


def fetch(index, sources, targets, sem):
    copies = []
    for i, (mine, other) in enumerate(sources):
        rows = mine.shape[0]
        for j, source in enumerate((mine, other)):
            at = pl.multiple_of((index if j == 0 else 1 - index) * rows, rows)
            copies.append(
                pltpu.make_async_copy(source, targets[i].at[pl.ds(at, rows)], sem.at[2 * i + j])
            )
    for copy in copies:
        copy.start()
    for copy in copies:
        copy.wait()


def weight_scratch(*shapes):
    return [pltpu.VMEM(shape, BF16) for shape in shapes] + [
        pltpu.SemaphoreType.DMA((2 * len(shapes),))
    ]


def tile4(values):
    return jnp.concatenate([values] * 4, axis=1)


def turn(values, cosine, sine):
    lane = lax.broadcasted_iota(jnp.int32, (values.shape[0], 128), 1)
    first = (lane & 63) < 32
    parts = []
    for c in range(4):
        u = values[:, c * 128 : (c + 1) * 128]
        swapped = jnp.where(first, pltpu.roll(u, 96, 1), pltpu.roll(u, 32, 1))
        parts.append(u * cosine + swapped * sine)
    return jnp.concatenate(parts, axis=1)


def head_masks():
    lane = lax.broadcasted_iota(jnp.int32, (1, 128), 1)
    return [((lane >> 6) == e).astype(F32).astype(BF16) for e in range(2)]


def feed_kernel(idx, x, gain, um, uo, dm, do, x1, a1, h1, g1, u, d, sem):
    @pl.when(pl.program_id(0) == 0)
    def _():
        fetch(idx[0], ((um, uo), (dm, do)), (u, d), sem)

    v = x[...].astype(F32)
    a = (norm(v)[0] * gain[...]).astype(BF16)
    a1[...] = a
    acc = None
    for j in range(4):
        c = slice(j * 512, (j + 1) * 512)
        z = dot(a, u[:, c])
        s = sigmoid(z)
        h = z * s
        g1[:, c] = (s + h * (1.0 - s)).astype(BF16)
        h = h.astype(BF16)
        h1[:, c] = h
        part = dot(h, d[c, :])
        acc = part if acc is None else acc + part
    x1[...] = v + 0.5 * acc


def attend_kernel(
    idx, x1, gain, cos, sin, segb, rows, jm, jo, om, oo,
    x2, a2, qo, ko, vo, pr, mixed, wj, wo, bias, sem,
):
    @pl.when(pl.program_id(0) == 0)
    def _():
        fetch(idx[0], ((jm, jo), (om, oo)), (wj, wo), sem)

    v = x1[0]
    a = (norm(v)[0] * gain[...]).astype(BF16)
    a2[0] = a
    cosine, sine = cos[0], sin[0]
    qo[0] = (turn(dot(a, wj[:, :512]), cosine, sine) * HDIM ** (-0.5)).astype(BF16)
    ko[0] = turn(dot(a, wj[:, 512:1024]), cosine, sine).astype(BF16)
    vo[0] = dot(a, wj[:, 1024:]).astype(BF16)
    size = bias.shape[0]
    row = lax.broadcasted_iota(jnp.int32, (size, size), 0)
    col = lax.broadcasted_iota(jnp.int32, (size, size), 1)
    allowed = (tile4(segb[0]) == rows[0, 0:1, :]) & ((rows[0, 1:2, :] > 0) | (row == col))
    bias[...] = jnp.where(allowed, 0.0, -1000000000.0)
    masks = head_masks()

    def pair(p, carry):
        c = pl.ds(pl.multiple_of(p * 128, 128), 128)
        q, k, val = qo[0, :, c], ko[0, :, c], vo[0, :, c]
        total = None
        for e in range(2):
            s = dot_nt(q * masks[e], k) + bias[...]
            ex = jnp.exp(s - jnp.max(s, axis=-1, keepdims=True))
            prob = (ex / jnp.sum(ex, axis=-1, keepdims=True)).astype(BF16)
            pr[0, 2 * p + e] = prob
            part = dot(prob, val * masks[e])
            total = part if total is None else total + part
        mixed[0, :, c] = total.astype(BF16)
        return carry

    lax.fori_loop(0, HEADS // 2, pair, 0)
    x2[0] = v + dot(mixed[0], wo[...])


def conv_taps(padded, shifts, fill):
    rows = shifts.shape[1]
    for b in range(8):
        shifts[b] = padded[b : b + rows, :]


def conv_kernel(
    idx, x2, gain, kern, validb, before, after, wm, wo,
    a3, glu, p1, p2, cout, stats, w, padded, shifts, sem,
):
    fetch(idx[0], ((wm, wo),), (w,), sem)
    a = (norm(x2[0])[0] * gain[...]).astype(BF16)
    a3[...] = a
    valid = tile4(validb[0])
    g1 = dot(a, w[:, :512])
    s = sigmoid(dot(a, w[:, 512:])) * valid
    g = g1 * s
    glu[...] = g
    p1[...] = s.astype(BF16)
    p2[...] = (g * (1.0 - s)).astype(BF16)
    size = g.shape[0]
    padded[0:PAD] = jnp.zeros((PAD, D), F32)
    padded[PAD : PAD + size] = g
    padded[PAD + size :] = jnp.zeros((padded.shape[0] - PAD - size, D), F32)
    conv_taps(padded, shifts, 0)
    chunk = 32

    def step(i, carry):
        r0 = pl.multiple_of(i * chunk, chunk)
        low, high = before[0, pl.ds(r0, chunk), :], after[0, pl.ds(r0, chunk), :]
        acc = [jnp.zeros((chunk, 128), F32) for _ in range(4)]
        for o in range(KER):
            shift_by = o - (KER - 1) // 2
            a8, b = divmod(shift_by + PAD, 8)
            if shift_by < 0:
                keep = low >= float(-shift_by)
            elif shift_by > 0:
                keep = high >= float(shift_by)
            for c in range(4):
                cs = slice(c * 128, (c + 1) * 128)
                value = shifts[b, pl.ds(r0 + 8 * a8, chunk), cs]
                if shift_by != 0:
                    value = jnp.where(keep, value, 0.0)
                acc[c] = acc[c] + kern[o : o + 1, cs] * value
        for c in range(4):
            cout[pl.ds(r0, chunk), c * 128 : (c + 1) * 128] = acc[c]
        return carry

    lax.fori_loop(0, size // chunk, step, 0)
    out = cout[...]
    weighted = out * valid
    stats[0:1] = column_sum(weighted)
    stats[1:2] = column_sum(weighted * out)
    stats[2:3] = column_sum(valid)
    stats[3:8] = jnp.zeros((5, D), F32)


def middle_kernel(
    idx, total, gains, conv, x2, og, cm, co, um, uo, dm, do,
    enc, a4, e3, a5, h2, dz, e4, db, dx3, sums, wc, u, d, deriv, sem,
):
    @pl.when(pl.program_id(0) == 0)
    def _():
        fetch(idx[0], ((cm, co), (um, uo), (dm, do)), (wc, u, d), sem)
        sums[...] = jnp.zeros(sums.shape, F32)

    gain_b, bias_b, gain_2, gain_f = (gains[i : i + 1] for i in range(4))
    count = total[2:3]
    mean = total[0:1] / count
    inverse = lax.rsqrt(total[1:2] / count - mean * mean + EPS)
    unit = (conv[...] - mean) * inverse
    act = unit * gain_b + bias_b
    s_act = sigmoid(act)
    a = (act * s_act).astype(BF16)
    a4[...] = a
    v3 = x2[0] + dot(a, wc[...])
    n5, inv5 = norm(v3)
    a = (n5 * gain_2).astype(BF16)
    a5[...] = a
    acc = None
    for j in range(4):
        c = slice(j * 512, (j + 1) * 512)
        z = dot(a, u[:, c])
        s = sigmoid(z)
        h = z * s
        deriv[:, c] = (s + h * (1.0 - s)).astype(BF16)
        h = h.astype(BF16)
        h2[:, c] = h
        part = dot(h, d[c, :])
        acc = part if acc is None else acc + part
    n6, inv6 = norm(v3 + 0.5 * acc)
    enc[...] = (n6 * gain_f).astype(BF16)
    dy = og[0].astype(F32)
    sums[3:4] += column_sum(dy * n6)
    grad4 = norm_back(dy, n6, inv6, gain_f)
    e = (0.5 * grad4).astype(BF16)
    e4[...] = e
    acc = None
    for j in range(4):
        c = slice(j * 512, (j + 1) * 512)
        g = (dot_nt(e, d[c, :]) * deriv[:, c].astype(F32)).astype(BF16)
        dz[:, c] = g
        part = dot_nt(g, u[:, c])
        acc = part if acc is None else acc + part
    sums[2:3] += column_sum(acc * n5)
    grad3 = grad4 + norm_back(acc, n5, inv5, gain_2)
    dx3[...] = grad3
    e = grad3.astype(BF16)
    e3[...] = e
    dact = dot_nt(e, wc[...]) * (s_act * (1.0 + act * (1.0 - s_act)))
    db[...] = dact
    sums[0:1] += column_sum(dact)
    sums[1:2] += column_sum(dact * unit)


def conv_back_kernel(
    idx, total, back, gains, kern, conv, db, glu, p1, p2, x2, dx3, validb, before, after, wm, wo,
    dg, dx2, e2, dk, sums, w, padded, shifts, dglu, dkacc, sem,
):
    fetch(idx[0], ((wm, wo),), (w,), sem)
    gain_b, gain_c = gains[0:1], gains[1:2]
    count = total[2:3]
    mean = total[0:1] / count
    inverse = lax.rsqrt(total[1:2] / count - mean * mean + EPS)
    valid = tile4(validb[0])
    unit = (conv[...] - mean) * inverse
    dc = inverse * (
        db[...] * gain_b - valid / count * (gain_b * back[0:1] + unit * (gain_b * back[1:2]))
    )
    size = dc.shape[0]
    padded[0:PAD] = jnp.zeros((PAD, D), F32)
    padded[PAD : PAD + size] = dc
    padded[PAD + size :] = jnp.zeros((padded.shape[0] - PAD - size, D), F32)
    conv_taps(padded, shifts, 0)
    dkacc[...] = jnp.zeros(dkacc.shape, F32)
    chunk = 32

    def step(i, carry):
        r0 = pl.multiple_of(i * chunk, chunk)
        low, high = before[0, pl.ds(r0, chunk), :], after[0, pl.ds(r0, chunk), :]
        for c in range(4):
            cs = slice(c * 128, (c + 1) * 128)
            own = glu[pl.ds(r0, chunk), cs]
            acc = jnp.zeros((chunk, 128), F32)
            for o in range(KER):
                shift_by = (KER - 1) // 2 - o
                a8, b = divmod(shift_by + PAD, 8)
                value = shifts[b, pl.ds(r0 + 8 * a8, chunk), cs]
                if shift_by < 0:
                    value = jnp.where(low >= float(-shift_by), value, 0.0)
                elif shift_by > 0:
                    value = jnp.where(high >= float(shift_by), value, 0.0)
                acc = acc + kern[o : o + 1, cs] * value
                prod = own * value
                part = prod[0:8]
                for q in range(1, chunk // 8):
                    part = part + prod[8 * q : 8 * q + 8]
                dkacc[o, :, cs] += part
            dglu[pl.ds(r0, chunk), cs] = acc
        return carry

    lax.fori_loop(0, size // chunk, step, 0)
    dk[...] = jnp.sum(dkacc[...], axis=1)
    grad = dglu[...]
    g1 = (grad * p1[...].astype(F32)).astype(BF16)
    g2 = (grad * p2[...].astype(F32)).astype(BF16)
    dg[:, :512] = g1
    dg[:, 512:] = g2
    da = dot_nt(g1, w[:, :512]) + dot_nt(g2, w[:, 512:])
    n3, inv3 = norm(x2[0])
    sums[0:1] = column_sum(da * n3)
    sums[1:8] = jnp.zeros((7, D), F32)
    out = dx3[...] + norm_back(da, n3, inv3, gain_c)
    dx2[...] = out
    e2[...] = out.astype(BF16)


def attend_back_kernel(
    idx, x1, gain, cos, sin, dx2a, dx2b, q, k, v, pr, jm, jo, om, oo,
    dj, dx1, e1, sums, wj, wo, dmix, dq, dkey, sem,
):
    micro = pl.program_id(0)

    @pl.when(micro == 0)
    def _():
        fetch(idx[0], ((jm, jo), (om, oo)), (wj, wo), sem)
        dx1[0] = dx2a[...]

    @pl.when(micro == 1)
    def _():
        dx1[0] = dx2b[...]

    grad2 = dx1[0]
    dmix[...] = dot_nt(grad2.astype(BF16), wo[...]).astype(BF16)
    masks = head_masks()

    def pair(p, carry):
        c = pl.ds(pl.multiple_of(p * 128, 128), 128)
        qp, kp, vp, gp = q[0, :, c], k[0, :, c], v[0, :, c], dmix[:, c]
        parts = [None, None, None]
        for e in range(2):
            prob = pr[0, 2 * p + e]
            grad = gp * masks[e]
            dp = dot_nt(grad, vp)
            wide = prob.astype(F32)
            prod = wide * dp
            ds = (prod - wide * jnp.sum(prod, axis=-1, keepdims=True)).astype(BF16)
            new = (dot(ds, kp * masks[e]), dot_tn(ds, qp * masks[e]), dot_tn(prob, grad))
            parts = [b if a is None else a + b for a, b in zip(parts, new)]
        dq[:, c] = parts[0]
        dkey[:, c] = parts[1]
        dj[0, :, pl.ds(pl.multiple_of(1024 + p * 128, 128), 128)] = parts[2].astype(BF16)
        return carry

    lax.fori_loop(0, HEADS // 2, pair, 0)
    cosine, sine = cos[0], -sin[0]
    dj[0, :, :512] = turn(dq[...] * HDIM ** (-0.5), cosine, sine).astype(BF16)
    dj[0, :, 512:1024] = turn(dkey[...], cosine, sine).astype(BF16)
    da = dot_nt(dj[0], wj[...])
    n2, inv2 = norm(x1[0])
    sums[0, 0:1] = column_sum(da * n2)
    sums[0, 1:8] = jnp.zeros((7, D), F32)
    out = grad2 + norm_back(da, n2, inv2, gain[...])
    dx1[0] = out
    e1[0] = (0.5 * out).astype(BF16)


def feed_back_kernel(idx, x, gain, dx1, e1, g1, um, uo, dm, do, fg, dz, sums, u, d, sem):
    @pl.when(pl.program_id(0) == 0)
    def _():
        fetch(idx[0], ((um, uo), (dm, do)), (u, d), sem)
        sums[...] = jnp.zeros(sums.shape, F32)

    e = e1[...]
    acc = None
    for j in range(4):
        c = slice(j * 512, (j + 1) * 512)
        g = (dot_nt(e, d[c, :]) * g1[:, c].astype(F32)).astype(BF16)
        dz[:, c] = g
        part = dot_nt(g, u[:, c])
        acc = part if acc is None else acc + part
    n1, inv1 = norm(x[...].astype(F32))
    sums[0:1] += column_sum(acc * n1)
    fg[...] = (dx1[...] + norm_back(acc, n1, inv1, gain[...])).astype(BF16)


def weight_kernel(plan, core, *refs):
    ins, (send, keep) = refs[:-2], refs[-2:]
    step = pl.program_id(0)

    def fill(out):
        at = 0
        for i, blocks in enumerate(plan):
            l0, r0, l1, r1 = ins[4 * i : 4 * i + 4]
            rows = l0.shape[1]
            for j in range(blocks):
                c = slice(j * 512, (j + 1) * 512)
                out[0, at : at + rows] = (
                    dot_tn(l0[...], r0[:, c]) + dot_tn(l1[...], r1[:, c])
                ).astype(BF16)
                at += rows

    @pl.when(step < 2)
    def _():
        fill(send)

    @pl.when(step >= 2)
    def _():
        fill(keep)


def full(shape):
    zeros = (0,) * len(shape)
    return pl.BlockSpec(shape, lambda *_: zeros)


def out(shape, dtype):
    return jax.ShapeDtypeStruct(shape, dtype)


def cost(flops, nbytes):
    return pl.CostEstimate(flops=int(flops), bytes_accessed=int(nbytes), transcendentals=0)


def micro_spec(shape, micro):
    rest = (0,) * len(shape)
    return pl.BlockSpec((1,) + shape, lambda *_: (micro,) + rest)


def weight_call(name, products, core):
    plan, specs, arrays, rows, flops = [], [], [], 0, 0

    def quarter(step, core_ref):
        x = step % 2
        mine = core_ref[0]
        return x * 2 + jnp.where(step < 2, 1 - mine, mine)

    for l0, r0, l1, r1 in products:
        slots, m = l0.shape
        n = r0.shape[1]
        plan.append(n // 512)
        rows += (n // 512) * (m // 4)
        flops += 4 * slots * m * n
        for left, right in ((l0, r0), (l1, r1)):
            specs.append(pl.BlockSpec((slots, m // 4), lambda s, ref: (0, quarter(s, ref))))
            specs.append(pl.BlockSpec((slots, n), lambda s, ref: (0, 0)))
            arrays += [left, right]
    nbytes = sum(a.size * 2 for a in arrays) + rows * 512 * 8
    return pl.pallas_call(
        functools.partial(weight_kernel, tuple(plan)),
        name=name,
        grid_spec=pltpu.PrefetchScalarGridSpec(
            num_scalar_prefetch=1,
            grid=(4,),
            in_specs=specs,
            out_specs=[
                pl.BlockSpec((1, rows, D), lambda s, ref: (jnp.minimum(s, 1), 0, 0)),
                pl.BlockSpec((1, rows, D), lambda s, ref: (jnp.maximum(s - 2, 0), 0, 0)),
            ],
        ),
        out_shape=[out((2, rows, D), BF16)] * 2,
        cost_estimate=cost(flops, nbytes),
    )(core, *arrays)


def unpack(reduced, shapes):
    found, at = [], 0
    for m, n in shapes:
        rows = (n // 512) * (m // 4)
        part = reduced[:, at : at + rows].astype(F32).reshape(2, n // 512, m // 4, 512)
        found.append(part.transpose(0, 2, 1, 3).reshape(m // 2, n))
        at += rows
    return found


def layout(lengths, mask, slots):
    ends = jnp.cumsum(lengths, axis=1)
    starts = ends - lengths
    slot = jnp.arange(slots, dtype=jnp.int32)
    reached = slot[None, :, None] >= ends[:, None, :]
    segment = jnp.sum(reached.astype(jnp.int32), axis=2)
    member = segment[:, :, None] == jnp.arange(lengths.shape[1], dtype=jnp.int32)
    begin = jnp.sum(jnp.where(member, starts[:, None, :], 0), axis=2)
    end = jnp.sum(jnp.where(member, ends[:, None, :], 0), axis=2)
    return segment, slot[None] - begin, end - 1 - slot[None]


def body(
    sizes, frames, item_lengths, frame_mask, first_norm, first_up, first_down, attend_norm,
    attend_joint, attend_out, conv_norm, conv_in, conv_kern, batch_gain, batch_bias, conv_out,
    second_norm, second_up, second_down, final_norm, output_grad,
):
    slots = frames.shape[1]
    x_at = lax.axis_index("fsdp").astype(jnp.int32).reshape(1)
    core = (lax.axis_index("dp") & 1).astype(jnp.int32).reshape(1)
    first_x = lax.axis_index("fsdp") == 0

    def other(shard):
        return swap(shard, "fsdp", 1, 2)

    norms = jnp.stack(
        [first_norm, attend_norm, conv_norm, batch_gain, batch_bias, second_norm, final_norm]
    )
    norms_o = other(norms)
    gains = jnp.concatenate(
        [jnp.where(first_x, norms, norms_o), jnp.where(first_x, norms_o, norms)], axis=1
    ).astype(F32)
    kern_o = other(conv_kern)
    kern = jnp.concatenate(
        [jnp.where(first_x, conv_kern, kern_o), jnp.where(first_x, kern_o, conv_kern)], axis=0
    ).astype(F32)
    up1, down1, joint, aout, cin, cout_w, up2, down2 = (
        (w, other(w))
        for w in (
            first_up, first_down, attend_joint, attend_out, conv_in, conv_out, second_up, second_down
        )
    )
    g_first, g_attend, g_conv, g_bn, b_bn, g_second, g_final = (
        gains[i : i + 1] for i in range(7)
    )
    segment, position, left = layout(item_lengths[:, 0], frame_mask, slots)
    half = HDIM // 2
    freq = jnp.exp(jnp.arange(half, dtype=F32) * (-2.0 * math.log(10000.0) / HDIM))
    angle = position.astype(F32)[:, :, None] * freq
    cosine, sine = jnp.cos(angle), jnp.sin(angle)
    cos_t = jnp.concatenate([cosine] * 4, axis=-1)
    sin_t = jnp.concatenate([-sine, sine, -sine, sine], axis=-1)
    valid = frame_mask.astype(F32)

    def wide(values):
        return jnp.broadcast_to(values.astype(F32)[:, :, None], (MB, slots, 128))

    segb, before, after, validb = wide(segment), wide(position), wide(left), wide(valid)
    rows = jnp.stack([segment.astype(F32), valid], axis=1)

    tall = MB * slots
    tm = 256
    x_flat = frames.reshape(tall, D)

    def row_spec(width):
        return pl.BlockSpec((tm, width), lambda i: (i, 0))

    x1, a1, h1, g1 = pl.pallas_call(
        feed_kernel,
        name="feed",
        grid=(tall // tm,),
        in_specs=[SMEM, row_spec(D), full((1, D)), ANY, ANY, ANY, ANY],
        out_specs=[row_spec(D), row_spec(D), row_spec(FF), row_spec(FF)],
        out_shape=[out((tall, D), F32), out((tall, D), BF16)] + [out((tall, FF), BF16)] * 2,
        scratch_shapes=weight_scratch((D, FF), (FF, D)),
        cost_estimate=cost(4 * tall * D * FF, 2e7),
    )(x_at, x_flat, g_first, *up1, *down1)

    def cut(array):
        return array.reshape(MB, slots, array.shape[-1])

    def by_micro(*shape):
        rest = (0,) * len(shape)
        return pl.BlockSpec((1,) + shape, lambda i: (i,) + rest)

    x1 = cut(x1)
    x2, a2, qh, kh, vh, probs, mixed = pl.pallas_call(
        attend_kernel,
        name="attend",
        grid=(MB,),
        in_specs=[
            SMEM, by_micro(slots, D), full((1, D)), by_micro(slots, 128), by_micro(slots, 128),
            by_micro(slots, 128), by_micro(2, slots), ANY, ANY, ANY, ANY,
        ],
        out_specs=[by_micro(slots, D)] * 5 + [by_micro(HEADS, slots, slots), by_micro(slots, D)],
        out_shape=[out((MB, slots, D), F32)] + [out((MB, slots, D), BF16)] * 4
        + [out((MB, HEADS, slots, slots), BF16), out((MB, slots, D), BF16)],
        scratch_shapes=[
            pltpu.VMEM((D, 3 * D), BF16), pltpu.VMEM((D, D), BF16), pltpu.VMEM((slots, slots), F32),
            pltpu.SemaphoreType.DMA((4,)),
        ],
        cost_estimate=cost(MB * slots * (8 * D * D + 8 * slots * D), 3e7),
    )(x_at, x1, g_attend, cos_t, sin_t, segb, rows, *joint, *aout)

    pad_rows = slots + 40

    def forward_conv(m):
        return pl.pallas_call(
            conv_kernel,
            name=f"conv_{m}",
            in_specs=[
                SMEM, micro_spec((slots, D), m), full((1, D)), full((KER, D)),
                *[micro_spec((slots, 128), m)] * 3, ANY, ANY,
            ],
            out_specs=[full((slots, D))] * 5 + [full((8, D))],
            grid=(1,),
            out_shape=[
                out((slots, D), BF16), out((slots, D), F32), out((slots, D), BF16),
                out((slots, D), BF16), out((slots, D), F32), out((8, D), F32),
            ],
            scratch_shapes=[
                pltpu.VMEM((D, 2 * D), BF16), pltpu.VMEM((pad_rows, D), F32),
                pltpu.VMEM((8, pad_rows - 8, D), F32), pltpu.SemaphoreType.DMA((2,)),
            ],
            cost_estimate=cost(4 * slots * D * D + 60 * KER * slots * D, 1e7),
        )(x_at, x2, g_conv, kern, validb, before, after, *cin)

    convs = [forward_conv(m) for m in range(MB)]
    totals = [sum_all(c[5], sizes) for c in convs]
    mid_gains = jnp.concatenate([g_bn, b_bn, g_second, g_final], axis=0)

    def middle(m):
        def at_micro(width):
            return pl.BlockSpec((1, tm, width), lambda i: (m, i, 0))

        return pl.pallas_call(
            middle_kernel,
            name=f"middle_{m}",
            grid=(slots // tm,),
            in_specs=[
                SMEM, full((8, D)), full((4, D)), row_spec(D), at_micro(D), at_micro(D),
                ANY, ANY, ANY, ANY, ANY, ANY,
            ],
            out_specs=[row_spec(D)] * 4 + [row_spec(FF)] * 2 + [row_spec(D)] * 3 + [full((8, D))],
            out_shape=[out((slots, D), BF16)] * 4 + [out((slots, FF), BF16)] * 2
            + [out((slots, D), BF16)] + [out((slots, D), F32)] * 2 + [out((8, D), F32)],
            scratch_shapes=[
                pltpu.VMEM((D, D), BF16), pltpu.VMEM((D, FF), BF16), pltpu.VMEM((FF, D), BF16),
                pltpu.VMEM((tm, FF), BF16), pltpu.SemaphoreType.DMA((6,)),
            ],
            cost_estimate=cost(slots * (8 * D * FF + 4 * D * D), 2e7),
        )(x_at, totals[m], mid_gains, convs[m][4], x2, output_grad, *cout_w, *up2, *down2)

    mids = [middle(m) for m in range(MB)]
    backs = [sum_all(mid[9], sizes) for mid in mids]
    enc = jnp.stack([mid[0] for mid in mids])

    def product(lefts, rights):
        return (lefts[0], rights[0], lefts[1], rights[1])

    a4, e3, a5, h2, dz2, e4 = ([mid[i] for mid in mids] for i in range(1, 7))
    send, keep = weight_call(
        "weights_second", [product(h2, e4), product(a5, dz2), product(a4, e3)], core
    )
    sum_second = reduce_rows(send, keep, sizes)
    back_gains = jnp.concatenate([g_bn, g_conv], axis=0)

    def back_conv(m):
        a3, glu, p1, p2, conv, _ = convs[m]
        return pl.pallas_call(
            conv_back_kernel,
            name=f"conv_back_{m}",
            grid=(1,),
            in_specs=[
                SMEM, full((8, D)), full((8, D)), full((2, D)), full((KER, D)),
                *[full((slots, D))] * 5, micro_spec((slots, D), m), full((slots, D)),
                *[micro_spec((slots, 128), m)] * 3, ANY, ANY,
            ],
            out_specs=[
                full((slots, 2 * D)), full((slots, D)), full((slots, D)), full((KER, D)), full((8, D)),
            ],
            out_shape=[
                out((slots, 2 * D), BF16), out((slots, D), F32), out((slots, D), BF16),
                out((KER, D), F32), out((8, D), F32),
            ],
            scratch_shapes=[
                pltpu.VMEM((D, 2 * D), BF16), pltpu.VMEM((pad_rows, D), F32),
                pltpu.VMEM((8, pad_rows - 8, D), F32), pltpu.VMEM((slots, D), F32),
                pltpu.VMEM((KER, 8, D), F32), pltpu.SemaphoreType.DMA((2,)),
            ],
            cost_estimate=cost(4 * slots * D * D + 120 * KER * slots * D, 1.5e7),
        )(x_at, totals[m], backs[m], back_gains, kern, conv, mids[m][7], glu, p1, p2, x2, mids[m][8],
          validb, before, after, *cin)

    conv_backs = [back_conv(m) for m in range(MB)]
    dj, dx1, e1, sums_attend = pl.pallas_call(
        attend_back_kernel,
        name="attend_back",
        grid=(MB,),
        in_specs=[
            SMEM, by_micro(slots, D), full((1, D)), by_micro(slots, 128), by_micro(slots, 128),
            full((slots, D)), full((slots, D)), *[by_micro(slots, D)] * 3,
            by_micro(HEADS, slots, slots), ANY, ANY, ANY, ANY,
        ],
        out_specs=[by_micro(slots, 3 * D), by_micro(slots, D), by_micro(slots, D), by_micro(8, D)],
        out_shape=[
            out((MB, slots, 3 * D), BF16), out((MB, slots, D), F32), out((MB, slots, D), BF16),
            out((MB, 8, D), F32),
        ],
        scratch_shapes=[
            pltpu.VMEM((D, 3 * D), BF16), pltpu.VMEM((D, D), BF16), pltpu.VMEM((slots, D), BF16),
            pltpu.VMEM((slots, D), F32), pltpu.VMEM((slots, D), F32), pltpu.SemaphoreType.DMA((4,)),
        ],
        cost_estimate=cost(MB * slots * (8 * D * D + 16 * slots * D), 3e7),
    )(x_at, x1, g_attend, cos_t, sin_t, conv_backs[0][1], conv_backs[1][1], qh, kh, vh, probs,
      *joint, *aout)
    send, keep = weight_call(
        "weights_attend",
        [
            product([c[0] for c in convs], [c[0] for c in conv_backs]),
            product(mixed, [c[2] for c in conv_backs]),
            product(a2, dj),
        ],
        core,
    )
    sum_attend = reduce_rows(send, keep, sizes)
    h1, a1 = cut(h1), cut(a1)
    send, keep = weight_call("weights_down", [product(h1, e1)], core)
    sum_down = reduce_rows(send, keep, sizes)
    fgrad, dz1, sums_first = pl.pallas_call(
        feed_back_kernel,
        name="feed_back",
        grid=(tall // tm,),
        in_specs=[
            SMEM, row_spec(D), full((1, D)), row_spec(D), row_spec(D), row_spec(FF), ANY, ANY, ANY, ANY,
        ],
        out_specs=[row_spec(D), row_spec(FF), full((8, D))],
        out_shape=[out((tall, D), BF16), out((tall, FF), BF16), out((8, D), F32)],
        scratch_shapes=weight_scratch((D, FF), (FF, D)),
        cost_estimate=cost(4 * tall * D * FF, 2e7),
    )(x_at, x_flat, g_first, dx1.reshape(tall, D), e1.reshape(tall, D), g1, *up1, *down1)
    dz1 = cut(dz1)
    send, keep = weight_call("weights_up", [product(a1, dz1)], core)
    sum_up = reduce_rows(send, keep, sizes)

    mid_sums = mids[0][9] + mids[1][9]
    small = jnp.concatenate(
        [
            conv_backs[0][3] + conv_backs[1][3],
            sums_first[0:1],
            sums_attend[0, 0:1] + sums_attend[1, 0:1],
            conv_backs[0][4][0:1] + conv_backs[1][4][0:1],
            mid_sums[1:2],
            mid_sums[0:1],
            mid_sums[2:4],
            jnp.zeros((1, D), F32),
        ],
        axis=0,
    )
    small = sum_all(small, sizes)
    kern_grad = lax.dynamic_slice_in_dim(small, x_at[0] * (KER // 2), KER // 2, axis=0)
    vectors = lax.dynamic_slice_in_dim(small[KER:], x_at[0] * (D // 2), D // 2, axis=1)

    down2_g, up2_g, cout_g = unpack(sum_second, [(FF, D), (D, FF), (D, D)])
    cin_g, aout_g, joint_g = unpack(sum_attend, [(D, 2 * D), (D, D), (D, 3 * D)])
    (down1_g,) = unpack(sum_down, [(FF, D)])
    (up1_g,) = unpack(sum_up, [(D, FF)])
    return (
        enc, fgrad.reshape(MB, slots, D), vectors[0], up1_g, down1_g, vectors[1], joint_g, aout_g,
        vectors[2], cin_g, kern_grad, vectors[3], vectors[4], cout_g, vectors[5], up2_g, down2_g,
        vectors[6],
    )


def solution(mesh):
    split = P(None, ("dp", "fsdp"), None)
    row, mat = P("fsdp"), P("fsdp", None)
    weights = (row, mat, mat, row, mat, mat, row, mat, mat, row, row, mat, row, mat, mat, row)
    return jax.shard_map(
        functools.partial(body, dict(mesh.shape)),
        mesh=mesh,
        in_specs=(split, split, P(None, ("dp", "fsdp"))) + weights + (split,),
        out_specs=(split, split) + weights,
        check_vma=False,
    )
```

time: 701 us -> 490 us (0.70)
  Pallas kernels: 0 us -> 190 us
  matrix products: 127 us -> 0 us
  waiting for transfers between devices: 273 us -> 150 us
  other arithmetic: 146 us -> 34.6 us
  local copies, waits for them, and re-layouts: 90.5 us -> 40.4 us
  starting transfers between devices: 54.6 us -> 68.4 us
    pallas_call x0 -> x14, Pallas kernels: none -> 190 us  [the longest x4 33.8 us: weight_call(): pl.pallas_call(functools.partial(weight_kernel, tuple(plan)), name=name,...]
    dot_general x60 -> x0, matrix products: 127 us -> none  [the longest x16 38.9 us: product_nt(): lax.dot_general(left, right, (((1,), (1,)), ((), ())), preferred_element_...]
    ppermute x50 -> x71, waiting for transfers between devices: 273 us -> 150 us  [swap(): return lax.ppermute(value, axis, [(i, i ^ bit) for i in range(size)])]
    reduce_sum x30 -> x2, other arithmetic: 44.8 us -> 0.19 us  [the longest x1 0.1 us: layout(): end = jnp.sum(jnp.where(member, ends[:, None, :], 0), axis=2)]
    unnamed x683 -> x43, local copies, waits for them, and re-layouts: 35.7 us -> 8.79 us
    reshape x8 -> x3, local copies, waits for them, and re-layouts: 24.4 us -> 2.97 us  [unpack(): found.append(part.transpose(0, 2, 1, 3).reshape(m // 2, n))]
    convert_element_type x22 -> x26, other arithmetic: 31.5 us -> 12.9 us  [the longest x16 9.8 us: add_split(): parts.append((left.astype(F32) + right.astype(F32)).astype(BF16))]
    another operation x21 -> x6, other arithmetic: 22 us -> 6.99 us  [the longest x3 3.42 us: unpack(): found.append(part.transpose(0, 2, 1, 3).reshape(m // 2, n))]
  transfers between devices with their start and end apart: 50 -> 71, of which waited for: 23 -> 30; matrix products, arithmetic and copies ran while one was open for 21% -> 12% of each run, Pallas kernels for 0% -> 25%
where the time goes in v2:
time: 490 us; the launch traced here: 486 us
  Pallas kernels  190 us (39%)
  waiting for transfers between devices  150 us (31%)
  starting transfers between devices  68.4 us (14%)
  local copies, waits for them, and re-layouts  40.4 us (8%)
  other arithmetic  34.6 us (7%)
    ppermute x71, waiting for transfers between devices, swap(): return lax.ppermute(value, axis, [(i, i ^ bit) for i in range(size)])  150 us
    ppermute x71, starting transfers between devices, swap(): return lax.ppermute(value, axis, [(i, i ^ bit) for i in range(size)])  68.4 us
    pallas_call x4, Pallas kernels, weight_call(): pl.pallas_call(functools.partial(weight_kernel, tuple(plan)), name=name,...  33.8 us
    pallas_call x2, Pallas kernels, back_conv(): pl.pallas_call(conv_back_kernel, name=f'conv_back_{m}', grid=(1,), in_spe...  29.4 us
    pallas_call x1, Pallas kernels, body(): pl.pallas_call(attend_back_kernel, name='attend_back', grid=(MB,), in_spe...  28.7 us
    pallas_call x2, Pallas kernels, middle(): pl.pallas_call(middle_kernel, name=f'middle_{m}', grid=(slots // tm,), in...  28.4 us
    pallas_call x1, Pallas kernels, body(): pl.pallas_call(attend_kernel, name='attend', grid=(MB,), in_specs=[SMEM,...  23.4 us
    pallas_call x2, Pallas kernels, forward_conv(): pl.pallas_call(conv_kernel, name=f'conv_{m}', in_specs=[SMEM, micro_spec(...  21.9 us
  transfers between devices with their start and end apart: 71, of which 30 were waited for; matrix products, arithmetic and copies ran while one was open for 12% of the time, Pallas kernels for 25%

profile of v2, /device:TPU:0, one launch (start us, length us, event | category | flops | bytes accessed | tf_op | source)
XLA Modules:
  0.0 485.6 jit_solution(3464771836000118176)
XLA Ops:
  5.3 3.0 collective-permute-start
  8.4 1.9 collective-permute-start.2
  10.4 1.9 collective-permute-start.4
  14.2 1.9 fusion.12
  20.6 57.8 %collective-permute-done.5 = bf16[16,512]{1,0:T(8,128)(2,1)S(1)} collective-permute-done((bf16[16,512]{1,0:T(8,128)(2,1)S(1)}, bf16[16,512]{1,0:T(8,128)(2,1)S(1)}, u32[]{:S(2)}, u32[]{:S(2)}) %collective-permute-start.5) | collective-permute-done | bytes 16416 | tf_op jit(solution)/shard_map/ppermute | solution.py:26
  79.5 1.6 collective-permute-start.13
  81.5 13.1 %feed.1 = (f32[1024,512]{1,0:T(8,128)}, bf16[1024,512]{1,0:T(8,128)(2,1)}, bf16[1024,2048]{1,0:T(8,128)(2,1)}, bf16[1024,2048]{1,0:T(8,128)(2,1)}) custom-call(s32[1]{0:T(128)} %bitcast.idx, bf16[1024,512]{1,0:T(8,128)(2,1)} %bitcast.141, f32[1,512]{1,0:T(1,128)} %get-tuple-element.299.gain, bf16[256,2048]{1,0:T(8,128)(2,1)} %um.7, ...), custom_call_target="tpu_custom_call" | custom-call | flops 4294967296 | bytes 20000000 | tf_op jit(solution)/shard_map/feed/pallas_call | solution.py:607
  94.6 1.7 collective-permute-start.12
  97.3 23.4 %attend.1 = (f32[2,512,512]{2,1,0:T(8,128)}, bf16[2,512,512]{2,1,0:T(8,128)(2,1)}, bf16[2,512,512]{2,1,0:T(8,128)(2,1)}, bf16[2,512,512]{2,1,0:T(8,128)(2,1)}, b...) custom-call(s32[1]{0:T(128)} %bitcast.idx, f32[2,512,512]{2,1,0:T(8,128)} %bitcast.143, ...), custom_call_target="tpu_custom_call" | custom-call | flops 4294967296 | bytes 30000000 | tf_op jit(solution)/shard_map/attend/pallas_call | solution.py:626
  123.8 11.0 %conv_1.1 = (bf16[512,512]{1,0:T(8,128)(2,1)}, f32[512,512]{1,0:T(8,128)}, bf16[512,512]{1,0:T(8,128)(2,1)}, bf16[512,512]{1,0:T(8,128)(2,1)}, f32[512,512]{1,0:T(8,128)}, /*index=5*/f32[8,512]{1,0:T(8,128)}) custom-call(s32[1]{0:T(128)} %bitcast.idx, f32[2,512,512]{2,1,0:T(8,128)} %get-tuple-element.87.x2, f32[1,512]{1,0:T(1,128)} %get-tuple-element.297.gain, ...), custom_call_target="tpu_custom_call" | custom-call | flops 1040187392 | bytes 10000000 | tf_op jit(solution)/shard_map/conv_1/pallas_call | solution.py:647
  134.9 11.0 %conv_0.1 = (bf16[512,512]{1,0:T(8,128)(2,1)}, f32[512,512]{1,0:T(8,128)}, bf16[512,512]{1,0:T(8,128)(2,1)}, bf16[512,512]{1,0:T(8,128)(2,1)}, f32[512,512]{1,0:T(8,128)}, /*index=5*/f32[8,512]{1,0:T(8,128)}) custom-call(s32[1]{0:T(128)} %bitcast.idx, f32[2,512,512]{2,1,0:T(8,128)} %get-tuple-element.87.x2, f32[1,512]{1,0:T(1,128)} %get-tuple-element.297.gain, ...), custom_call_target="tpu_custom_call" | custom-call | flops 1040187392 | bytes 10000000 | tf_op jit(solution)/shard_map/conv_0/pallas_call | solution.py:647
  154.2 2.6 collective-permute-start.18
  156.8 2.1 collective-permute-start.10
  163.3 14.4 %middle_1.1 = (bf16[512,512]{1,0:T(8,128)(2,1)}, bf16[512,512]{1,0:T(8,128)(2,1)}, bf16[512,512]{1,0:T(8,128)(2,1)}, bf16[512,512]{1,0:T(8,128)(2,1)}, bf16[512,...) custom-call(s32[1]{0:T(128)} %bitcast.idx, ...), custom_call_target="tpu_custom_call" | custom-call | flops 4831838208 | bytes 20000000 | tf_op jit(solution)/shard_map/middle_1/pallas_call | solution.py:675
  178.4 14.0 %middle_0.1 = (bf16[512,512]{1,0:T(8,128)(2,1)}, bf16[512,512]{1,0:T(8,128)(2,1)}, bf16[512,512]{1,0:T(8,128)(2,1)}, bf16[512,512]{1,0:T(8,128)(2,1)}, bf16[512,...) custom-call(s32[1]{0:T(128)} %bitcast.idx, ...), custom_call_target="tpu_custom_call" | custom-call | flops 4831838208 | bytes 20000000 | tf_op jit(solution)/shard_map/middle_0/pallas_call | solution.py:675
  192.9 5.0 %fusion.14 = (bf16[512,2048]{1,0:T(8,128)(2,1)}, bf16[512,2048]{1,0:T(8,128)(2,1)}) fusion(bf16[1024,2048]{1,0:T(8,128)(2,1)} %get-tuple-element.126), kind=kLoop, calls=%fused_computation.142 | loop fusion | bytes 8388608 | tf_op jit(solution)/shard_map/slice | solution.py:698
  201.8 1.6 collective-permute-start.22
  205.7 2.7 collective-permute-start.23
  211.4 1.7 collective-permute-done.28
  215.2 1.7 collective-permute-done.29
  217.5 14.7 %conv_back_0.1 = (bf16[512,1024]{1,0:T(8,128)(2,1)}, f32[512,512]{1,0:T(8,128)}, bf16[512,512]{1,0:T(8,128)(2,1)}, f32[32,512]{1,0:T(8,128)}, f32[8,512]{1,0:T(8,128)}) custom-call(s32[1]{0:T(128)} %bitcast.idx, f32[8,512]{1,0:T(8,128)} %add.308.total, f32[8,512]{1,0:T(8,128)} %add.318.back, f32[2,512]{1,0:T(2,128)} %pad_maximum_fusion.19.gains, ...), custom_call_target="tpu_custom_call" | custom-call | flops 1543503872 | bytes 15000000 | tf_op jit(solution)/shard_map/conv_back_0/pallas_call | solution.py:709
  232.1 14.7 %conv_back_1.1 = (bf16[512,1024]{1,0:T(8,128)(2,1)}, f32[512,512]{1,0:T(8,128)}, bf16[512,512]{1,0:T(8,128)(2,1)}, f32[32,512]{1,0:T(8,128)}, f32[8,512]{1,0:T(8,128)}) custom-call(s32[1]{0:T(128)} %bitcast.idx, f32[8,512]{1,0:T(8,128)} %add.313.total, f32[8,512]{1,0:T(8,128)} %add.323.back, f32[2,512]{1,0:T(2,128)} %pad_maximum_fusion.19.gains, ...), custom_call_target="tpu_custom_call" | custom-call | flops 1543503872 | bytes 15000000 | tf_op jit(solution)/shard_map/conv_back_1/pallas_call | solution.py:709
  246.8 28.7 %attend_back.1 = (bf16[2,512,1536]{2,1,0:T(8,128)(2,1)}, f32[2,512,512]{2,1,0:T(8,128)}, bf16[2,512,512]{2,1,0:T(8,128)(2,1)}, f32[2,8,512]{2,1,0:T(8,128)}) custom-call(s32[1]{0:T(128)} %bitcast.idx, f32[2,512,512]{2,1,0:T(8,128)} %bitcast.144, f32[1,512]{1,0:T(1,128)} %get-tuple-element.298.gain, f32[2,512,128]{2,1,0:T(8,128)} %pad_maximum_fusion.7.cos, ...), custom_call_target="tpu_custom_call" | custom-call | flops 6442450944 | bytes 30000000 | tf_op jit(solution)/shard_map/attend_back/pallas_call | solution.py:735
  275.5 2.2 slice_bitcast_fusion.6
  277.8 11.6 %feed_back.1 = (bf16[1024,512]{1,0:T(8,128)(2,1)}, bf16[1024,2048]{1,0:T(8,128)(2,1)}, f32[8,512]{1,0:T(8,128)}) custom-call(s32[1]{0:T(128)} %bitcast.idx, bf16[1024,512]{1,0:T(8,128)(2,1)} %bitcast.142, f32[1,512]{1,0:T(1,128)} %get-tuple-element.299.gain, f32[1024,512]{1,0:T(8,128)} %bitcast.145, bf16[1024,512]{1,0:T(8,128)(2,1)} %bitcast.129, ...), custom_call_target="tpu_custom_call" | custom-call | flops 4294967296 | bytes 20000000 | tf_op jit(solution)/shard_map/feed_back/pallas_call | solution.py:769
  291.7 4.8 fusion.15
  296.5 7.1 %weights_up.1 = (bf16[2,512,512]{2,1,0:T(8,128)(2,1)}, bf16[2,512,512]{2,1,0:T(8,128)(2,1)}) custom-call(s32[1]{0:T(128)} %bitcast.14.core, bf16[512,512]{1,0:T(8,128)(2,1)} %get-tuple-element.253.refs_0_, bf16[512,2048]{1,0:T(8,128)(2,1)} %get-tuple-element.215.refs_1_, bf16[512,512]{1,0:T(8,128)(2,1)} %get-tuple-element.252.refs_2_, ...), custom_call_target="tpu_custom_call" | custom-call | flops 2147483648 | bytes 7340032 | tf_op jit(solution)/shard_map/weights_up/pallas_call | solution.py:513
  304.1 6.4 %weights_down.1 = (bf16[2,512,512]{2,1,0:T(8,128)(2,1)}, bf16[2,512,512]{2,1,0:T(8,128)(2,1)}) custom-call(s32[1]{0:T(128)} %bitcast.14.core, bf16[512,2048]{1,0:T(8,128)(2,1)} %get-tuple-element.213.refs_0_, bf16[512,512]{1,0:T(8,128)(2,1)} %get-tuple-element.247.refs_1_, bf16[512,2048]{1,0:T(8,128)(2,1)} %get-tuple-element.212.refs_2_, ...), custom_call_target="tpu_custom_call" | custom-call | flops 2147483648 | bytes 7340032 | tf_op jit(solution)/shard_map/weights_down/pallas_call | solution.py:513
  311.7 1.9 slice_bitcast_fusion
  313.5 1.9 collective-permute-done.31
  316.7 9.2 %weights_attend.1 = (bf16[2,768,512]{2,1,0:T(8,128)(2,1)}, bf16[2,768,512]{2,1,0:T(8,128)(2,1)}) custom-call(s32[1]{0:T(128)} %bitcast.14.core, bf16[512,512]{1,0:T(8,128)(2,1)} %get-tuple-element.129.refs_0_, bf16[512,1024]{1,0:T(8,128)(2,1)} %get-tuple-element.130.refs_1_, bf16[512,512]{1,0:T(8,128)(2,1)} %get-tuple-element.131.refs_2_, ...), custom_call_target="tpu_custom_call" | custom-call | flops 3221225472 | bytes 12582912 | tf_op jit(solution)/shard_map/weights_attend/pallas_call | solution.py:513
  326.1 1.7 collective-permute-start.33
  327.8 2.6 add_convert_fusion.7
  331.0 2.6 add_convert_fusion.5
  335.1 11.2 %weights_second.1 = (bf16[2,1152,512]{2,1,0:T(8,128)(2,1)}, bf16[2,1152,512]{2,1,0:T(8,128)(2,1)}) custom-call(s32[1]{0:T(128)} %bitcast.14.core, bf16[512,2048]{1,0:T(8,128)(2,1)} %get-tuple-element.140.refs_0_, bf16[512,512]{1,0:T(8,128)(2,1)} %get-tuple-element.141.refs_1_, bf16[512,2048]{1,0:T(8,128)(2,1)} %get-tuple-element.142.refs_2_, ...), custom_call_target="tpu_custom_call" | custom-call | flops 4831838208 | bytes 17301504 | tf_op jit(solution)/shard_map/weights_second/pallas_call | solution.py:513
  347.0 2.1 pad_maximum_fusion.3
  349.1 8.5 %collective-permute-done.34 = f32[40,512]{1,0:T(8,128)S(1)} collective-permute-done((f32[40,512]{1,0:T(8,128)S(1)}, f32[40,512]{1,0:T(8,128)S(1)}, u32[]{:S(2)}, u32[]{:S(2)}) %collective-permute-start.34) | collective-permute-done | bytes 81952 | tf_op jit(solution)/shard_map/ppermute | solution.py:26
  360.6 1.7 collective-permute-start.46
  363.6 4.6 collective-permute-done.37
  368.7 3.4 collective-permute-done.46
  375.6 2.0 collective-permute-done.47
  377.6 1.9 collective-permute-start.48
  379.5 2.2 collective-permute-done.39
  381.9 2.5 collective-permute-done.48
  385.0 2.1 collective-permute-done.40
  387.5 2.5 collective-permute-done.49
  392.3 1.8 collective-permute-start.42
  397.6 3.9 collective-permute-done.42
  401.8 6.4 %collective-permute-done.55 = bf16[384,512]{1,0:T(8,128)(2,1)S(1)} collective-permute-done((bf16[384,512]{1,0:T(8,128)(2,1)S(1)}, bf16[384,512]{1,0:T(8,128)(2,1)S(1)}, u32[]{:S(2)}, u32[]{:S(2)}) %collective-permute-start.55) | collective-permute-done | bytes 393248 | tf_op jit(solution)/shard_map/ppermute | solution.py:26
  408.3 7.8 %collective-permute-done.63 = bf16[1152,512]{1,0:T(8,128)(2,1)S(1)} collective-permute-done((bf16[1152,512]{1,0:T(8,128)(2,1)S(1)}, bf16[1152,512]{1,0:T(8,128)(2,1)S(1)}, u32[]{:S(2)}, u32[]{:S(2)}) %collective-permute-start.63) | collective-permute-done | bytes 1179680 | tf_op jit(solution)/shard_map/ppermute | solution.py:26
  419.8 8.1 %collective-permute-done.64 = bf16[576,512]{1,0:T(8,128)(2,1)S(1)} collective-permute-done((bf16[576,512]{1,0:T(8,128)(2,1)S(1)}, bf16[576,512]{1,0:T(8,128)(2,1)S(1)}, u32[]{:S(2)}, u32[]{:S(2)}) %collective-permute-start.64) | collective-permute-done | bytes 589856 | tf_op jit(solution)/shard_map/ppermute | solution.py:26
  429.8 1.9 collective-permute-start.58
  431.7 7.5 %collective-permute-done.65 = bf16[288,512]{1,0:T(8,128)(2,1)S(1)} collective-permute-done((bf16[288,512]{1,0:T(8,128)(2,1)S(1)}, bf16[288,512]{1,0:T(8,128)(2,1)S(1)}, u32[]{:S(2)}, u32[]{:S(2)}) %collective-permute-start.65) | collective-permute-done | bytes 294944 | tf_op jit(solution)/shard_map/ppermute | solution.py:26
  439.9 2.5 collective-permute-start.59
  442.4 4.7 collective-permute-done.66
  448.2 2.0 collective-permute-start.60
  450.2 4.3 collective-permute-done.67
  455.1 6.3 %collective-permute-done.68 = bf16[288,512]{1,0:T(8,128)(2,1)S(1)} collective-permute-done((bf16[288,512]{1,0:T(8,128)(2,1)S(1)}, bf16[288,512]{1,0:T(8,128)(2,1)S(1)}, u32[]{:S(2)}, u32[]{:S(2)}) %collective-permute-start.68) | collective-permute-done | bytes 294944 | tf_op jit(solution)/shard_map/ppermute | solution.py:26
  463.8 2.2 copy.62
  466.0 1.6 maximum_convert_fusion
  467.6 3.8 collective-permute-done.69
  473.7 2.1 copy.63
  481.3 2.2 copy.65
  483.5 1.7 bitcast_convert_fusion
  (277 shorter events, 83.8 us)
Async XLA Ops:
  5.3 14.7 %collective-permute-start = (bf16[7,256]{1,0:T(8,128)(2,1)S(1)}, bf16[7,256]{1,0:T(8,128)(2,1)S(1)}, u32[]{:S(2)}, u32[]{:S(2)}) collective-permute-start(bf16[7,256]{1,0:T(8,128)(2,1)S(1)} %stack.47), channel_id=1, source_target_pairs={{0,1},{1,0},{2,3},{3,2},{4,5},{5,4},{6,7},{7,6},{8,9},{9,8},{10,11... | collective-permute-start | bytes 10760 | tf_op jit(solution)/shard_map/ppermute | solution.py:26
  8.3 71.2 %collective-permute-start.1 = (bf16[256,2048]{1,0:T(8,128)(2,1)}, bf16[256,2048]{1,0:T(8,128)(2,1)}, u32[]{:S(2)}, u32[]{:S(2)}) collective-permute-start(bf16[256,2048]{1,0:T(8,128)(2,1)} %um.7), channel_id=1, source_target_pairs={{0,1},{1,0},{2,3},{3,2},{4,5},{5,4},{6,7},{7,6},{8,9},{9,8},{10,11... | collective-permute-start | bytes 3145736 | tf_op jit(solution)/shard_map/ppermute | solution.py:26
  8.4 72.7 %collective-permute-start.2 = (bf16[1024,512]{1,0:T(8,128)(2,1)}, bf16[1024,512]{1,0:T(8,128)(2,1)}, u32[]{:S(2)}, u32[]{:S(2)}) collective-permute-start(bf16[1024,512]{1,0:T(8,128)(2,1)} %dm.7), channel_id=1, source_target_pairs={{0,1},{1,0},{2,3},{3,2},{4,5},{5,4},{6,7},{7,6},{8,9},{9,8},{10,11... | collective-permute-start | bytes 3145736 | tf_op jit(solution)/shard_map/ppermute | solution.py:26
  10.3 86.0 %collective-permute-start.3 = (bf16[256,1536]{1,0:T(8,128)(2,1)}, bf16[256,1536]{1,0:T(8,128)(2,1)}, u32[]{:S(2)}, u32[]{:S(2)}) collective-permute-start(bf16[256,1536]{1,0:T(8,128)(2,1)} %jm.3), channel_id=1, source_target_pairs={{0,1},{1,0},{2,3},{3,2},{4,5},{5,4},{6,7},{7,6},{8,9},{9,8},{10,11... | collective-permute-start | bytes 2359304 | tf_op jit(solution)/shard_map/ppermute | solution.py:26
  10.4 84.2 %collective-permute-start.4 = (bf16[256,512]{1,0:T(8,128)(2,1)}, bf16[256,512]{1,0:T(8,128)(2,1)}, u32[]{:S(2)}, u32[]{:S(2)}) collective-permute-start(bf16[256,512]{1,0:T(8,128)(2,1)} %om.3), channel_id=1, source_target_pairs={{0,1},{1,0},{2,3},{3,2},{4,5},{5,4},{6,7},{7,6},{8,9},{9,8},{10,11... | collective-permute-start | bytes 786440 | tf_op jit(solution)/shard_map/ppermute | solution.py:26
  20.0 58.5 %collective-permute-start.5 = (bf16[16,512]{1,0:T(8,128)(2,1)S(1)}, bf16[16,512]{1,0:T(8,128)(2,1)S(1)}, u32[]{:S(2)}, u32[]{:S(2)}) collective-permute-start(bf16[16,512]{1,0:T(8,128)(2,1)S(1)} %copy-done.15), channel_id=1, source_target_pairs={{0,1},{1,0},{2,3},{3,2},{4,5},{5,4},{6,7},{7,6},{8,9},{9,8},{10,11... | collective-permute-start | bytes 49160 | tf_op jit(solution)/shard_map/ppermute | solution.py:26
  78.4 42.3 %collective-permute-start.6 = (bf16[256,1024]{1,0:T(8,128)(2,1)S(1)}, bf16[256,1024]{1,0:T(8,128)(2,1)S(1)}, u32[]{:S(2)}, u32[]{:S(2)}) collective-permute-start(bf16[256,1024]{1,0:T(8,128)(2,1)S(1)} %copy-done), channel_id=1, source_target_pairs={{0,1},{1,0},{2,3},{3,2},{4,5},{5,4},{6,7},{7,6},{8,9},{9,8},{10,11... | collective-permute-start | bytes 1572872 | tf_op jit(solution)/shard_map/ppermute | solution.py:26
  79.5 83.8 %collective-permute-start.13 = (bf16[256,2048]{1,0:T(8,128)(2,1)S(1)}, bf16[256,2048]{1,0:T(8,128)(2,1)}, u32[]{:S(2)}, u32[]{:S(2)}) collective-permute-start(bf16[256,2048]{1,0:T(8,128)(2,1)S(1)} %copy-done.16), channel_id=1, source_target_pairs={{0,1},{1,0},{2,3},{3,2},{4,5},{5,4},{6,7},{7,6},{8,9},{9,8},{10,11... | collective-permute-start | bytes 3145736 | tf_op jit(solution)/shard_map/ppermute | solution.py:26
  81.1 82.1 %collective-permute-start.14 = (bf16[1024,512]{1,0:T(8,128)(2,1)S(1)}, bf16[1024,512]{1,0:T(8,128)(2,1)}, u32[]{:S(2)}, u32[]{:S(2)}) collective-permute-start(bf16[1024,512]{1,0:T(8,128)(2,1)S(1)} %copy-done.17), channel_id=1, source_target_pairs={{0,1},{1,0},{2,3},{3,2},{4,5},{5,4},{6,7},{7,6},{8,9},{9,8},{10,11... | collective-permute-start | bytes 3145736 | tf_op jit(solution)/shard_map/ppermute | solution.py:26
  94.6 68.6 %collective-permute-start.12 = (bf16[256,512]{1,0:T(8,128)(2,1)S(1)}, bf16[256,512]{1,0:T(8,128)(2,1)}, u32[]{:S(2)}, u32[]{:S(2)}) collective-permute-start(bf16[256,512]{1,0:T(8,128)(2,1)S(1)} %copy-done.18), channel_id=1, source_target_pairs={{0,1},{1,0},{2,3},{3,2},{4,5},{5,4},{6,7},{7,6},{8,9},{9,8},{10,11... | collective-permute-start | bytes 786440 | tf_op jit(solution)/shard_map/ppermute | solution.py:26
  134.8 11.6 %collective-permute-start.15 = (f32[8,512]{1,0:T(8,128)}, f32[8,512]{1,0:T(8,128)S(1)}, u32[]{:S(2)}, u32[]{:S(2)}) collective-permute-start(f32[8,512]{1,0:T(8,128)} %get-tuple-element.91), channel_id=1, source_target_pairs={{0,2},{2,0},{4,6},{6,4},{8,10},{10,8},{12,14},{14,12},{16,18},{18,... | collective-permute-start | bytes 49160 | tf_op jit(solution)/shard_map/ppermute | solution.py:26
  150.2 3.9 collective-permute-start.17
  152.5 4.3 collective-permute-start.9
  154.2 4.7 collective-permute-start.18
  156.8 4.7 collective-permute-start.10
  161.5 16.3 %collective-permute-start.11 = (f32[8,512]{1,0:T(8,128)S(1)}, f32[8,512]{1,0:T(8,128)S(1)}, u32[]{:S(2)}, u32[]{:S(2)}) collective-permute-start(f32[8,512]{1,0:T(8,128)S(1)} %add.307), channel_id=1, source_target_pairs={{0,1},{1,0},{2,3},{3,2},{4,5},{5,4},{6,7},{7,6},{8,9},{9,8},{10,11... | collective-permute-start | bytes 49160 | tf_op jit(solution)/shard_map/ppermute | solution.py:26
  177.7 20.2 %collective-permute-start.25 = (f32[8,512]{1,0:T(8,128)}, f32[8,512]{1,0:T(8,128)S(1)}, u32[]{:S(2)}, u32[]{:S(2)}) collective-permute-start(f32[8,512]{1,0:T(8,128)} %get-tuple-element.101), channel_id=1, source_target_pairs={{0,2},{2,0},{4,6},{6,4},{8,10},{10,8},{12,14},{14,12},{16,18},{18,... | collective-permute-start | bytes 49160 | tf_op jit(solution)/shard_map/ppermute | solution.py:26
  192.3 5.5 %collective-permute-start.20 = (f32[8,512]{1,0:T(8,128)}, f32[8,512]{1,0:T(8,128)S(1)}, u32[]{:S(2)}, u32[]{:S(2)}) collective-permute-start(f32[8,512]{1,0:T(8,128)} %get-tuple-element.94), channel_id=1, source_target_pairs={{0,2},{2,0},{4,6},{6,4},{8,10},{10,8},{12,14},{14,12},{16,18},{18,... | collective-permute-start | bytes 49160 | tf_op jit(solution)/shard_map/ppermute | solution.py:26
  199.4 4.0 collective-permute-start.26
  201.8 3.9 collective-permute-start.22
  203.4 5.0 %collective-permute-start.27 = (f32[8,512]{1,0:T(8,128)S(1)}, f32[8,512]{1,0:T(8,128)S(1)}, u32[]{:S(2)}, u32[]{:S(2)}) collective-permute-start(f32[8,512]{1,0:T(8,128)S(1)} %add.320), channel_id=1, source_target_pairs={{0,8},{2,10},{4,12},{6,14},{8,0},{10,2},{12,4},{14,6},{16,24},{18,... | collective-permute-start | bytes 49160 | tf_op jit(solution)/shard_map/ppermute | solution.py:26
  205.7 5.1 %collective-permute-start.23 = (f32[8,512]{1,0:T(8,128)S(1)}, f32[8,512]{1,0:T(8,128)S(1)}, u32[]{:S(2)}, u32[]{:S(2)}) collective-permute-start(f32[8,512]{1,0:T(8,128)S(1)} %add.316), channel_id=1, source_target_pairs={{0,16},{2,18},{4,20},{6,22},{8,24},{10,26},{12,28},{14,30},{16,0},... | collective-permute-start | bytes 49160 | tf_op jit(solution)/shard_map/ppermute | solution.py:26
  208.4 4.7 collective-permute-start.28
  291.6 19.0 %collective-permute-start.30 = (f32[40,512]{1,0:T(8,128)S(1)}, f32[40,512]{1,0:T(8,128)S(1)}, u32[]{:S(2)}, u32[]{:S(2)}) collective-permute-start(f32[40,512]{1,0:T(8,128)S(1)} %concatenate.72), channel_id=1, source_target_pairs={{0,2},{2,0},{4,6},{6,4},{8,10},{10,8},{12,14},{14,12},{16,18},{18,... | collective-permute-start | bytes 245768 | tf_op jit(solution)/shard_map/ppermute | solution.py:26
  303.6 24.3 %collective-permute-start.35 = (bf16[2,512,512]{2,1,0:T(8,128)(2,1)}, bf16[2,512,512]{2,1,0:T(8,128)(2,1)}, u32[]{:S(2)}, u32[]{:S(2)}) collective-permute-start(bf16[2,512,512]{2,1,0:T(8,128)(2,1)} %get-tuple-element.125), channel_id=1, source_target_pairs={{0,2},{2,0},{4,6},{6,4},{8,10},{10,8},{12,14},{14,12},{16,18},{18,... | collective-permute-start | bytes 3145736 | tf_op jit(solution)/shard_map/ppermute | solution.py:26
  310.5 20.5 %collective-permute-start.44 = (bf16[2,512,512]{2,1,0:T(8,128)(2,1)}, bf16[2,512,512]{2,1,0:T(8,128)(2,1)}, u32[]{:S(2)}, u32[]{:S(2)}) collective-permute-start(bf16[2,512,512]{2,1,0:T(8,128)(2,1)} %get-tuple-element.128), channel_id=1, source_target_pairs={{0,2},{2,0},{4,6},{6,4},{8,10},{10,8},{12,14},{14,12},{16,18},{18,... | collective-permute-start | bytes 3145736 | tf_op jit(solution)/shard_map/ppermute | solution.py:26
  310.6 4.9 collective-permute-start.31
  315.5 10.7 %collective-permute-start.32 = (f32[40,512]{1,0:T(8,128)S(1)}, f32[40,512]{1,0:T(8,128)S(1)}, u32[]{:S(2)}, u32[]{:S(2)}) collective-permute-start(f32[40,512]{1,0:T(8,128)S(1)} %add.330), channel_id=1, source_target_pairs={{0,8},{2,10},{4,12},{6,14},{8,0},{10,2},{12,4},{14,6},{16,24},{18,... | collective-permute-start | bytes 245768 | tf_op jit(solution)/shard_map/ppermute | solution.py:26
  326.0 46.7 %collective-permute-start.53 = (bf16[2,768,512]{2,1,0:T(8,128)(2,1)}, bf16[2,768,512]{2,1,0:T(8,128)(2,1)S(1)}, u32[]{:S(2)}, u32[]{:S(2)}) collective-permute-start(bf16[2,768,512]{2,1,0:T(8,128)(2,1)} %get-tuple-element.139), channel_id=1, source_target_pairs={{0,2},{2,0},{4,6},{6,4},{8,10},{10,8},{12,14},{14,12},{16,18},{18,... | collective-permute-start | bytes 4718600 | tf_op jit(solution)/shard_map/ppermute | solution.py:26
  326.1 20.2 %collective-permute-start.33 = (f32[40,512]{1,0:T(8,128)S(1)}, f32[40,512]{1,0:T(8,128)S(1)}, u32[]{:S(2)}, u32[]{:S(2)}) collective-permute-start(f32[40,512]{1,0:T(8,128)S(1)} %add.331), channel_id=1, source_target_pairs={{0,16},{2,18},{4,20},{6,22},{8,24},{10,26},{12,28},{14,30},{16,0},... | collective-permute-start | bytes 245768 | tf_op jit(solution)/shard_map/ppermute | solution.py:26
  330.4 27.2 %collective-permute-start.36 = (bf16[512,512]{1,0:T(8,128)(2,1)}, bf16[512,512]{1,0:T(8,128)(2,1)}, u32[]{:S(2)}, u32[]{:S(2)}) collective-permute-start(bf16[512,512]{1,0:T(8,128)(2,1)} %get-tuple-element.229), channel_id=1, source_target_pairs={{0,1},{1,0},{2,3},{3,2},{4,5},{5,4},{6,7},{7,6},{8,9},{9,8},{10,11... | collective-permute-start | bytes 1572872 | tf_op jit(solution)/shard_map/ppermute | solution.py:26
  333.6 25.8 %collective-permute-start.45 = (bf16[512,512]{1,0:T(8,128)(2,1)}, bf16[512,512]{1,0:T(8,128)(2,1)}, u32[]{:S(2)}, u32[]{:S(2)}) collective-permute-start(bf16[512,512]{1,0:T(8,128)(2,1)} %get-tuple-element.227), channel_id=1, source_target_pairs={{0,1},{1,0},{2,3},{3,2},{4,5},{5,4},{6,7},{7,6},{8,9},{9,8},{10,11... | collective-permute-start | bytes 1572872 | tf_op jit(solution)/shard_map/ppermute | solution.py:26
  346.2 44.2 %collective-permute-start.62 = (bf16[2,1152,512]{2,1,0:T(8,128)(2,1)}, bf16[2,1152,512]{2,1,0:T(8,128)(2,1)S(1)}, u32[]{:S(2)}, u32[]{:S(2)}) collective-permute-start(bf16[2,1152,512]{2,1,0:T(8,128)(2,1)} %get-tuple-element.153), channel_id=1, source_target_pairs={{0,2},{2,0},{4,6},{6,4},{8,10},{10,8},{12,14},{14,12},{16,18},{18,... | collective-permute-start | bytes 7077896 | tf_op jit(solution)/shard_map/ppermute | solution.py:26
  346.3 11.3 %collective-permute-start.34 = (f32[40,512]{1,0:T(8,128)S(1)}, f32[40,512]{1,0:T(8,128)S(1)}, u32[]{:S(2)}, u32[]{:S(2)}) collective-permute-start(f32[40,512]{1,0:T(8,128)S(1)} %add.332), channel_id=1, source_target_pairs={{0,1},{1,0},{2,3},{3,2},{4,5},{5,4},{6,7},{7,6},{8,9},{9,8},{10,11... | collective-permute-start | bytes 245768 | tf_op jit(solution)/shard_map/ppermute | solution.py:26
  359.0 9.2 %collective-permute-start.37 = (bf16[256,512]{1,0:T(8,128)(2,1)S(1)}, bf16[256,512]{1,0:T(8,128)(2,1)S(1)}, u32[]{:S(2)}, u32[]{:S(2)}) collective-permute-start(bf16[256,512]{1,0:T(8,128)(2,1)S(1)} %get-tuple-element.251), channel_id=1, source_target_pairs={{0,4},{2,6},{4,0},{6,2},{8,12},{10,14},{12,8},{14,10},{16,20},{18,... | collective-permute-start | bytes 786440 | tf_op jit(solution)/shard_map/ppermute | solution.py:26
  360.6 11.6 %collective-permute-start.46 = (bf16[256,512]{1,0:T(8,128)(2,1)S(1)}, bf16[256,512]{1,0:T(8,128)(2,1)S(1)}, u32[]{:S(2)}, u32[]{:S(2)}) collective-permute-start(bf16[256,512]{1,0:T(8,128)(2,1)S(1)} %get-tuple-element.245), channel_id=1, source_target_pairs={{0,4},{2,6},{4,0},{6,2},{8,12},{10,14},{12,8},{14,10},{16,20},{18,... | collective-permute-start | bytes 786440 | tf_op jit(solution)/shard_map/ppermute | solution.py:26
  368.3 5.7 %collective-permute-start.38 = (bf16[128,512]{1,0:T(8,128)(2,1)S(1)}, bf16[128,512]{1,0:T(8,128)(2,1)S(1)}, u32[]{:S(2)}, u32[]{:S(2)}) collective-permute-start(bf16[128,512]{1,0:T(8,128)(2,1)S(1)} %get-tuple-element.267), channel_id=1, source_target_pairs={{0,8},{2,10},{4,12},{6,14},{8,0},{10,2},{12,4},{14,6},{16,24},{18,... | collective-permute-start | bytes 393224 | tf_op jit(solution)/shard_map/ppermute | solution.py:26
  372.2 5.3 %collective-permute-start.47 = (bf16[128,512]{1,0:T(8,128)(2,1)S(1)}, bf16[128,512]{1,0:T(8,128)(2,1)S(1)}, u32[]{:S(2)}, u32[]{:S(2)}) collective-permute-start(bf16[128,512]{1,0:T(8,128)(2,1)S(1)} %get-tuple-element.263), channel_id=1, source_target_pairs={{0,8},{2,10},{4,12},{6,14},{8,0},{10,2},{12,4},{14,6},{16,24},{18,... | collective-permute-start | bytes 393224 | tf_op jit(solution)/shard_map/ppermute | solution.py:26
  373.1 22.1 %collective-permute-start.54 = (bf16[768,512]{1,0:T(8,128)(2,1)S(1)}, bf16[768,512]{1,0:T(8,128)(2,1)S(1)}, u32[]{:S(2)}, u32[]{:S(2)}) collective-permute-start(bf16[768,512]{1,0:T(8,128)(2,1)S(1)} %get-tuple-element.217), channel_id=1, source_target_pairs={{0,1},{1,0},{2,3},{3,2},{4,5},{5,4},{6,7},{7,6},{8,9},{9,8},{10,11... | collective-permute-start | bytes 2359304 | tf_op jit(solution)/shard_map/ppermute | solution.py:26
  374.0 7.7 %collective-permute-start.39 = (bf16[64,512]{1,0:T(8,128)(2,1)S(1)}, bf16[64,512]{1,0:T(8,128)(2,1)S(1)}, u32[]{:S(2)}, u32[]{:S(2)}) collective-permute-start(bf16[64,512]{1,0:T(8,128)(2,1)S(1)} %add_convert_fusion.26), channel_id=1, source_target_pairs={{0,16},{2,18},{4,20},{6,22},{8,24},{10,26},{12,28},{14,30},{16,0},... | collective-permute-start | bytes 196616 | tf_op jit(solution)/shard_map/ppermute | solution.py:26
  377.6 6.8 %collective-permute-start.48 = (bf16[64,512]{1,0:T(8,128)(2,1)S(1)}, bf16[64,512]{1,0:T(8,128)(2,1)S(1)}, u32[]{:S(2)}, u32[]{:S(2)}) collective-permute-start(bf16[64,512]{1,0:T(8,128)(2,1)S(1)} %add_convert_fusion.23), channel_id=1, source_target_pairs={{0,16},{2,18},{4,20},{6,22},{8,24},{10,26},{12,28},{14,30},{16,0},... | collective-permute-start | bytes 196616 | tf_op jit(solution)/shard_map/ppermute | solution.py:26
  381.8 5.3 %collective-permute-start.40 = (bf16[64,512]{1,0:T(8,128)(2,1)S(1)}, bf16[64,512]{1,0:T(8,128)(2,1)S(1)}, u32[]{:S(2)}, u32[]{:S(2)}) collective-permute-start(bf16[64,512]{1,0:T(8,128)(2,1)S(1)} %add_convert_fusion.25), channel_id=1, source_target_pairs={{0,16},{2,18},{4,20},{6,22},{8,24},{10,26},{12,28},{14,30},{16,0},... | collective-permute-start | bytes 196616 | tf_op jit(solution)/shard_map/ppermute | solution.py:26
  384.4 5.7 %collective-permute-start.49 = (bf16[64,512]{1,0:T(8,128)(2,1)S(1)}, bf16[64,512]{1,0:T(8,128)(2,1)S(1)}, u32[]{:S(2)}, u32[]{:S(2)}) collective-permute-start(bf16[64,512]{1,0:T(8,128)(2,1)S(1)} %add_convert_fusion.22), channel_id=1, source_target_pairs={{0,16},{2,18},{4,20},{6,22},{8,24},{10,26},{12,28},{14,30},{16,0},... | collective-permute-start | bytes 196616 | tf_op jit(solution)/shard_map/ppermute | solution.py:26
  387.1 5.1 %collective-permute-start.41 = (bf16[128,512]{1,0:T(8,128)(2,1)S(1)}, bf16[128,512]{1,0:T(8,128)(2,1)S(1)}, u32[]{:S(2)}, u32[]{:S(2)}) collective-permute-start(bf16[128,512]{1,0:T(8,128)(2,1)S(1)} %pad_maximum_fusion.16), channel_id=1, source_target_pairs={{0,8},{2,10},{4,12},{6,14},{8,0},{10,2},{12,4},{14,6},{16,24},{18,... | collective-permute-start | bytes 393224 | tf_op jit(solution)/shard_map/ppermute | solution.py:26
  390.1 5.0 %collective-permute-start.50 = (bf16[128,512]{1,0:T(8,128)(2,1)S(1)}, bf16[128,512]{1,0:T(8,128)(2,1)S(1)}, u32[]{:S(2)}, u32[]{:S(2)}) collective-permute-start(bf16[128,512]{1,0:T(8,128)(2,1)S(1)} %pad_maximum_fusion.17), channel_id=1, source_target_pairs={{0,8},{2,10},{4,12},{6,14},{8,0},{10,2},{12,4},{14,6},{16,24},{18,... | collective-permute-start | bytes 393224 | tf_op jit(solution)/shard_map/ppermute | solution.py:26
  391.1 25.0 %collective-permute-start.63 = (bf16[1152,512]{1,0:T(8,128)(2,1)S(1)}, bf16[1152,512]{1,0:T(8,128)(2,1)S(1)}, u32[]{:S(2)}, u32[]{:S(2)}) collective-permute-start(bf16[1152,512]{1,0:T(8,128)(2,1)S(1)} %get-tuple-element.211), channel_id=1, source_target_pairs={{0,1},{1,0},{2,3},{3,2},{4,5},{5,4},{6,7},{7,6},{8,9},{9,8},{10,11... | collective-permute-start | bytes 3538952 | tf_op jit(solution)/shard_map/ppermute | solution.py:26
  392.3 9.2 %collective-permute-start.42 = (bf16[256,512]{1,0:T(8,128)(2,1)S(1)}, bf16[256,512]{1,0:T(8,128)(2,1)S(1)}, u32[]{:S(2)}, u32[]{:S(2)}) collective-permute-start(bf16[256,512]{1,0:T(8,128)(2,1)S(1)} %pad_maximum_fusion.13), channel_id=1, source_target_pairs={{0,4},{2,6},{4,0},{6,2},{8,12},{10,14},{12,8},{14,10},{16,20},{18,... | collective-permute-start | bytes 786440 | tf_op jit(solution)/shard_map/ppermute | solution.py:26
  395.4 12.7 %collective-permute-start.55 = (bf16[384,512]{1,0:T(8,128)(2,1)S(1)}, bf16[384,512]{1,0:T(8,128)(2,1)S(1)}, u32[]{:S(2)}, u32[]{:S(2)}) collective-permute-start(bf16[384,512]{1,0:T(8,128)(2,1)S(1)} %get-tuple-element.233), channel_id=1, source_target_pairs={{0,4},{2,6},{4,0},{6,2},{8,12},{10,14},{12,8},{14,10},{16,20},{18,... | collective-permute-start | bytes 1179656 | tf_op jit(solution)/shard_map/ppermute | solution.py:26
  397.0 21.0 %collective-permute-start.51 = (bf16[256,512]{1,0:T(8,128)(2,1)S(1)}, bf16[256,512]{1,0:T(8,128)(2,1)S(1)}, u32[]{:S(2)}, u32[]{:S(2)}) collective-permute-start(bf16[256,512]{1,0:T(8,128)(2,1)S(1)} %pad_maximum_fusion.14), channel_id=1, source_target_pairs={{0,4},{2,6},{4,0},{6,2},{8,12},{10,14},{12,8},{14,10},{16,20},{18,... | collective-permute-start | bytes 786440 | tf_op jit(solution)/shard_map/ppermute | solution.py:26
  401.7 17.9 %collective-permute-start.43 = (bf16[512,512]{1,0:T(8,128)(2,1)S(1)}, bf16[512,512]{1,0:T(8,128)(2,1)S(1)}, u32[]{:S(2)}, u32[]{:S(2)}) collective-permute-start(bf16[512,512]{1,0:T(8,128)(2,1)S(1)} %pad_maximum_fusion.9), channel_id=1, source_target_pairs={{0,2},{2,0},{4,6},{6,4},{8,10},{10,8},{12,14},{14,12},{16,18},{18,... | collective-permute-start | bytes 1572872 | tf_op jit(solution)/shard_map/ppermute | solution.py:26
  408.2 9.9 %collective-permute-start.56 = (bf16[192,512]{1,0:T(8,128)(2,1)S(1)}, bf16[192,512]{1,0:T(8,128)(2,1)S(1)}, u32[]{:S(2)}, u32[]{:S(2)}) collective-permute-start(bf16[192,512]{1,0:T(8,128)(2,1)S(1)} %get-tuple-element.257), channel_id=1, source_target_pairs={{0,8},{2,10},{4,12},{6,14},{8,0},{10,2},{12,4},{14,6},{16,24},{18,... | collective-permute-start | bytes 589832 | tf_op jit(solution)/shard_map/ppermute | solution.py:26
  416.4 11.5 %collective-permute-start.64 = (bf16[576,512]{1,0:T(8,128)(2,1)S(1)}, bf16[576,512]{1,0:T(8,128)(2,1)S(1)}, u32[]{:S(2)}, u32[]{:S(2)}) collective-permute-start(bf16[576,512]{1,0:T(8,128)(2,1)S(1)} %get-tuple-element.225), channel_id=1, source_target_pairs={{0,4},{2,6},{4,0},{6,2},{8,12},{10,14},{12,8},{14,10},{16,20},{18,... | collective-permute-start | bytes 1769480 | tf_op jit(solution)/shard_map/ppermute | solution.py:26
  418.1 44.2 %collective-permute-start.52 = (bf16[512,512]{1,0:T(8,128)(2,1)S(1)}, bf16[512,512]{1,0:T(8,128)(2,1)S(1)}, u32[]{:S(2)}, u32[]{:S(2)}) collective-permute-start(bf16[512,512]{1,0:T(8,128)(2,1)S(1)} %pad_maximum_fusion.10), channel_id=1, source_target_pairs={{0,2},{2,0},{4,6},{6,4},{8,10},{10,8},{12,14},{14,12},{16,18},{18,... | collective-permute-start | bytes 1572872 | tf_op jit(solution)/shard_map/ppermute | solution.py:26
  418.2 11.5 %collective-permute-start.57 = (bf16[96,512]{1,0:T(8,128)(2,1)S(1)}, bf16[96,512]{1,0:T(8,128)(2,1)S(1)}, u32[]{:S(2)}, u32[]{:S(2)}) collective-permute-start(bf16[96,512]{1,0:T(8,128)(2,1)S(1)} %add_convert_fusion.20), channel_id=1, source_target_pairs={{0,16},{2,18},{4,20},{6,22},{8,24},{10,26},{12,28},{14,30},{16,0},... | collective-permute-start | bytes 294920 | tf_op jit(solution)/shard_map/ppermute | solution.py:26
  428.1 11.2 %collective-permute-start.65 = (bf16[288,512]{1,0:T(8,128)(2,1)S(1)}, bf16[288,512]{1,0:T(8,128)(2,1)S(1)}, u32[]{:S(2)}, u32[]{:S(2)}) collective-permute-start(bf16[288,512]{1,0:T(8,128)(2,1)S(1)} %get-tuple-element.237), channel_id=1, source_target_pairs={{0,8},{2,10},{4,12},{6,14},{8,0},{10,2},{12,4},{14,6},{16,24},{18,... | collective-permute-start | bytes 884744 | tf_op jit(solution)/shard_map/ppermute | solution.py:26
  429.8 10.1 %collective-permute-start.58 = (bf16[96,512]{1,0:T(8,128)(2,1)S(1)}, bf16[96,512]{1,0:T(8,128)(2,1)S(1)}, u32[]{:S(2)}, u32[]{:S(2)}) collective-permute-start(bf16[96,512]{1,0:T(8,128)(2,1)S(1)} %add_convert_fusion.19), channel_id=1, source_target_pairs={{0,16},{2,18},{4,20},{6,22},{8,24},{10,26},{12,28},{14,30},{16,0},... | collective-permute-start | bytes 294920 | tf_op jit(solution)/shard_map/ppermute | solution.py:26
  439.3 7.9 %collective-permute-start.66 = (bf16[144,512]{1,0:T(8,128)(2,1)S(1)}, bf16[144,512]{1,0:T(8,128)(2,1)S(1)}, u32[]{:S(2)}, u32[]{:S(2)}) collective-permute-start(bf16[144,512]{1,0:T(8,128)(2,1)S(1)} %add_convert_fusion.13), channel_id=1, source_target_pairs={{0,16},{2,18},{4,20},{6,22},{8,24},{10,26},{12,28},{14,30},{16,0},... | collective-permute-start | bytes 442376 | tf_op jit(solution)/shard_map/ppermute | solution.py:26
  439.9 8.3 %collective-permute-start.59 = (bf16[192,512]{1,0:T(8,128)(2,1)S(1)}, bf16[192,512]{1,0:T(8,128)(2,1)S(1)}, u32[]{:S(2)}, u32[]{:S(2)}) collective-permute-start(bf16[192,512]{1,0:T(8,128)(2,1)S(1)} %pad_maximum_fusion.15), channel_id=1, source_target_pairs={{0,8},{2,10},{4,12},{6,14},{8,0},{10,2},{12,4},{14,6},{16,24},{18,... | collective-permute-start | bytes 589832 | tf_op jit(solution)/shard_map/ppermute | solution.py:26
  447.2 7.3 %collective-permute-start.67 = (bf16[144,512]{1,0:T(8,128)(2,1)S(1)}, bf16[144,512]{1,0:T(8,128)(2,1)S(1)}, u32[]{:S(2)}, u32[]{:S(2)}) collective-permute-start(bf16[144,512]{1,0:T(8,128)(2,1)S(1)} %add_convert_fusion.12), channel_id=1, source_target_pairs={{0,16},{2,18},{4,20},{6,22},{8,24},{10,26},{12,28},{14,30},{16,0},... | collective-permute-start | bytes 442376 | tf_op jit(solution)/shard_map/ppermute | solution.py:26
  448.2 13.7 %collective-permute-start.60 = (bf16[384,512]{1,0:T(8,128)(2,1)S(1)}, bf16[384,512]{1,0:T(8,128)(2,1)S(1)}, u32[]{:S(2)}, u32[]{:S(2)}) collective-permute-start(bf16[384,512]{1,0:T(8,128)(2,1)S(1)} %pad_maximum_fusion.11), channel_id=1, source_target_pairs={{0,4},{2,6},{4,0},{6,2},{8,12},{10,14},{12,8},{14,10},{16,20},{18,... | collective-permute-start | bytes 1179656 | tf_op jit(solution)/shard_map/ppermute | solution.py:26
  454.6 6.8 %collective-permute-start.68 = (bf16[288,512]{1,0:T(8,128)(2,1)S(1)}, bf16[288,512]{1,0:T(8,128)(2,1)S(1)}, u32[]{:S(2)}, u32[]{:S(2)}) collective-permute-start(bf16[288,512]{1,0:T(8,128)(2,1)S(1)} %pad_maximum_fusion.12), channel_id=1, source_target_pairs={{0,8},{2,10},{4,12},{6,14},{8,0},{10,2},{12,4},{14,6},{16,24},{18,... | collective-permute-start | bytes 884744 | tf_op jit(solution)/shard_map/ppermute | solution.py:26
  461.5 9.9 %collective-permute-start.69 = (bf16[576,512]{1,0:T(8,128)(2,1)S(1)}, bf16[576,512]{1,0:T(8,128)(2,1)S(1)}, u32[]{:S(2)}, u32[]{:S(2)}) collective-permute-start(bf16[576,512]{1,0:T(8,128)(2,1)S(1)} %pad_maximum_fusion.6), channel_id=1, source_target_pairs={{0,4},{2,6},{4,0},{6,2},{8,12},{10,14},{12,8},{14,10},{16,20},{18,... | collective-permute-start | bytes 1769480 | tf_op jit(solution)/shard_map/ppermute | solution.py:26
  462.1 9.7 %collective-permute-start.61 = (bf16[768,512]{1,0:T(8,128)(2,1)S(1)}, bf16[768,512]{1,0:T(8,128)(2,1)S(1)}, u32[]{:S(2)}, u32[]{:S(2)}) collective-permute-start(bf16[768,512]{1,0:T(8,128)(2,1)S(1)} %pad_maximum_fusion.5), channel_id=1, source_target_pairs={{0,2},{2,0},{4,6},{6,4},{8,10},{10,8},{12,14},{14,12},{16,18},{18,... | collective-permute-start | bytes 2359304 | tf_op jit(solution)/shard_map/ppermute | solution.py:26
  471.8 7.0 %collective-permute-start.70 = (bf16[1152,512]{1,0:T(8,128)(2,1)S(1)}, bf16[1152,512]{1,0:T(8,128)(2,1)S(1)}, u32[]{:S(2)}, u32[]{:S(2)}) collective-permute-start(bf16[1152,512]{1,0:T(8,128)(2,1)S(1)} %pad_maximum_fusion.2), channel_id=1, source_target_pairs={{0,2},{2,0},{4,6},{6,4},{8,10},{10,8},{12,14},{14,12},{16,18},{18,... | collective-permute-start | bytes 3538952 | tf_op jit(solution)/shard_map/ppermute | solution.py:26
  (26 other events, 391.6 us)
